TPU v7x, 32 devices: a whole 2x2x4 slice. The times are simulated.
32 devices in a mesh: seq: 8 (over z, y), tp: 4 (over x, core).
Axes of the slice: x: 2, y: 2, z: 4, core: 2. Of those that a mesh axis runs over, the one named last changes fastest.
Arguments:
- hidden: bfloat16 [1024, 4096], P('seq', 'tp'), may hold values from -6 to 6
- w_proj: bfloat16 [4096, 1024], P('tp'), may hold values from -1 to 1
- codes: int32 [1024, 4], P('seq'), may hold values from 0 to 2047
- embed_table: bfloat16 [3, 2048, 1024], P(None, None, 'tp'), may hold values from -6 to 6
- w_qkv: bfloat16 [1024, 3, 1024], P(None, None, 'tp'), may hold values from -1 to 1
- w_out: bfloat16 [1024, 1024], P('tp'), may hold values from -0.1875 to 0.1875
- head_table: bfloat16 [4, 1024, 2048], P(None, None, 'tp'), may hold values from -1 to 1
- gain_attn: float32 [1024], replicated, may hold values from 0.5 to 1.5
- gain_head: float32 [1024], replicated, may hold values from 0.5 to 1.5
Outputs:
- row_loss: float32 [1024, 4], P('seq')
- grad_hidden: bfloat16 [1024, 4096], P('seq', 'tp')
- grad_proj: float32 [4096, 1024], P('tp', 'seq')
All inputs are finite; a program needn't handle non-finite values.
Results may differ from a plain program's by a relative error of at most 0.02.
Values may be sent and summed in bfloat16 or wider, within the bound.
No kernel may reach another device: no remote copies, remote signals or barrier semaphores. Data moves between devices by JAX's collectives and lax.ppermute only.
A program may use at most 64 MiB of HBM per device.

v0:
```python
import functools

import jax
import jax.numpy as jnp
from jax import lax
from jax.experimental import pallas as pl
from jax.experimental.pallas import tpu as pltpu
from jax.sharding import PartitionSpec as P


HEADS = 16
EPS = 1e-06
ROWS = 16
F32 = jnp.float32
BF16 = jnp.bfloat16


def dot(a, b):
    return lax.dot_general(a, b, (((1,), (0,)), ((), ())), preferred_element_type=F32)


def dot_t(a, b):
    return lax.dot_general(a, b, (((1,), (1,)), ((), ())), preferred_element_type=F32)


def inverse_rms(stream):
    return lax.rsqrt(jnp.mean(stream * stream, axis=-1, keepdims=True) + EPS)


def norm_back(stream, gain, cotangent):
    inverse = inverse_rms(stream)
    scaled = gain * cotangent
    along = jnp.mean(stream * scaled, axis=-1, keepdims=True)
    return inverse * scaled - stream * (inverse * inverse * inverse * along)


def head_ones(lanes, head_dim):
    rows = lax.broadcasted_iota(jnp.int32, (lanes, lanes), 0) // head_dim
    columns = lax.broadcasted_iota(jnp.int32, (lanes, lanes), 1) // head_dim
    return jnp.where(rows == columns, 1.0, 0.0).astype(BF16)


def pairs_of(steps):
    return [(a, b) for a in range(steps) for b in range(a + 1)]


def call(kernel, outs, scratch, args, cost, spaces=None, limit=16):
    specs = [pl.BlockSpec(memory_space=pltpu.VMEM) for _ in args]
    for place, space in (spaces or {}).items():
        specs[place] = pl.BlockSpec(memory_space=space)
    return pl.pallas_call(
        kernel,
        out_shape=[jax.ShapeDtypeStruct(shape, dtype) for shape, dtype in outs],
        in_specs=specs,
        out_specs=[pl.BlockSpec(memory_space=pltpu.VMEM) for _ in outs],
        scratch_shapes=scratch,
        cost_estimate=pl.CostEstimate(flops=cost, bytes_accessed=cost // 300, transcendentals=0),
        compiler_params=pltpu.CompilerParams(vmem_limit_bytes=limit * 1024 * 1024),
    )(*args)


def chunk(index):
    return pl.ds(pl.multiple_of(index * ROWS, ROWS), ROWS)


def at_row(base, index):
    return pl.ds(pl.multiple_of(base + index * ROWS, ROWS), ROWS)


def cut_kernel(weight_ref, out_ref):
    rows = out_ref.shape[0]
    place = lax.axis_index("seq") % 2 * rows
    out_ref[...] = weight_ref[pl.ds(pl.multiple_of(place, rows), rows), :]


def lookup_kernel(codes_ref, table_ref, mine_ref, other_ref):
    count, half = mine_ref.shape[:2]
    vocab = table_ref.shape[1]
    core = lax.axis_index("tp") % 2
    low = codes_ref[pl.ds(pl.multiple_of(core * half, half), half), :]
    high = codes_ref[pl.ds(pl.multiple_of((1 - core) * half, half), half), :]
    codes = jnp.concatenate([low, high], axis=0)
    lanes = lax.broadcasted_iota(jnp.int32, (2 * half, vocab), 1)
    for k in range(count):
        chosen = jnp.where(lanes == codes[:, k : k + 1], 1.0, 0.0).astype(BF16)
        found = dot(chosen, table_ref[k]).astype(BF16)
        mine_ref[k] = found[:half]
        other_ref[k] = found[half:]


def context_kernel(hidden_ref, weight_ref, mine_ref, other_ref):
    half = mine_ref.shape[0]
    core = lax.axis_index("tp") % 2
    low = hidden_ref[pl.ds(pl.multiple_of(core * half, half), half), :]
    high = hidden_ref[pl.ds(pl.multiple_of((1 - core) * half, half), half), :]
    partial = dot(jnp.concatenate([low, high], axis=0), weight_ref[...])
    mine_ref[...] = partial[:half]
    other_ref[...] = partial[half:].astype(BF16)


def attention_kernel(
    head_dim, own_ref, side_ref, look0, look1, look2, look3, qkv_mine, qkv_pair, gain_ref,
    stream_ref, att_ref, proj_mine, proj_pair, soft_mine, soft_pair,
    look_ref, normed_ref, product_ref, score_ref,
):
    steps, half, _ = stream_ref.shape
    rank = lax.axis_index("tp")
    lanes = look0.shape[2]
    chunks = half // ROWS
    pairs = pairs_of(steps)
    scale = head_dim ** (-0.5)
    for j, look in enumerate((look0, look1, look2, look3)):
        place = pl.ds(pl.multiple_of((rank ^ j) * lanes, lanes), lanes)
        for k in range(steps - 1):
            look_ref[k, :, place] = look[k]

    def enter(i, carry):
        context = own_ref[chunk(i), :].astype(F32) + side_ref[chunk(i), :].astype(F32)
        for k in range(steps):
            stream = context if k == 0 else context + look_ref[k - 1, chunk(i), :].astype(F32)
            stream_ref[k, chunk(i), :] = stream
            normed = stream * inverse_rms(stream) * gain_ref[...]
            normed_ref[at_row(k * half, i), :] = normed.astype(BF16)
        return carry

    lax.fori_loop(0, chunks, enter, 0)
    ones = head_ones(lanes, head_dim)
    for j, (weight, proj, soft) in enumerate(
        ((qkv_mine, proj_mine, soft_mine), (qkv_pair, proj_pair, soft_pair))
    ):
        for part in range(3):
            proj[:, part * lanes : (part + 1) * lanes] = dot(normed_ref[...], weight[part]).astype(BF16)

        def multiply(i, carry):
            rows = [at_row(k * half, i) for k in range(steps)]
            query = [proj[row, 0:lanes] for row in rows]
            keys = [proj[row, lanes : 2 * lanes] for row in rows]
            for p, (a, b) in enumerate(pairs):
                product_ref[at_row(p * half, i), :] = query[a] * keys[b]
            return carry

        lax.fori_loop(0, chunks, multiply, 0)
        score_ref[...] = dot(product_ref[...], ones) * scale

        def weigh(i, carry):
            rows = [at_row(k * half, i) for k in range(steps)]
            values = [proj[row, 2 * lanes : 3 * lanes].astype(F32) for row in rows]
            for a in range(steps):
                first = pairs.index((a, 0))
                row = [score_ref[at_row((first + b) * half, i), :] for b in range(a + 1)]
                top = functools.reduce(jnp.maximum, row)
                row = [jnp.exp(item - top) for item in row]
                total = functools.reduce(jnp.add, row)
                mixed = 0.0
                for b in range(a + 1):
                    weight_ab = row[b] / total
                    soft[at_row((first + b) * half, i), :] = weight_ab
                    mixed = mixed + weight_ab.astype(BF16).astype(F32) * values[b]
                att_ref[rows[a], j * lanes : (j + 1) * lanes] = mixed.astype(BF16)
            return carry

        lax.fori_loop(0, chunks, weigh, 0)


def head_kernel(
    att_mine, att_theirs, own_ref, pair_ref, part_a, part_b, part_c, part_d, stream_ref, gain_ref, codes_ref, head_mine, head_pair,
    mid_ref, expo_ref, stats_ref, full_ref, mixed_ref, normed_ref, logit_ref,
):
    steps, half, _ = stream_ref.shape
    rank = lax.axis_index("tp")
    core = rank % 2
    vocab = head_mine.shape[2]
    chunks = half // ROWS
    lanes, cut = own_ref.shape[0], part_a.shape[0]
    place = lax.axis_index("seq") % 2
    full_ref[0:lanes, :] = own_ref[...]
    full_ref[lanes : 2 * lanes, :] = pair_ref[...]
    for base, first, second in ((2 * lanes, part_a, part_b), (3 * lanes, part_c, part_d)):
        full_ref[pl.ds(pl.multiple_of(base + place * cut, cut), cut), :] = first[...]
        full_ref[pl.ds(pl.multiple_of(base + (1 - place) * cut, cut), cut), :] = second[...]
    mixed_ref[...] = dot(att_mine[...], full_ref[0 : 2 * lanes, :]) + dot(
        att_theirs[...], full_ref[2 * lanes : 4 * lanes, :]
    )

    def enter(i, carry):
        for k in range(steps):
            stream = stream_ref[k, chunk(i), :] + mixed_ref[at_row(k * half, i), :]
            mid_ref[k, chunk(i), :] = stream
            normed = stream * inverse_rms(stream) * gain_ref[...]
            normed_ref[at_row(k * half, i), :] = normed.astype(BF16)
        return carry

    lax.fori_loop(0, chunks, enter, 0)
    for k in range(steps):
        normed = normed_ref[k * half : (k + 1) * half, :]
        logit_ref[k, :, 0:vocab] = dot(normed, head_mine[k])
        logit_ref[k, :, vocab : 2 * vocab] = dot(normed, head_pair[k])

    def leave(i, carry):
        lanes = lax.broadcasted_iota(jnp.int32, (ROWS, 2 * vocab), 1)
        ids = jnp.where(lanes < vocab, lanes + rank * vocab, lanes - vocab + (rank ^ 1) * vocab)
        spots = lax.broadcasted_iota(jnp.int32, (ROWS, stats_ref.shape[1]), 1)
        stats = jnp.zeros((ROWS, stats_ref.shape[1]), F32)
        codes = codes_ref[pl.ds(pl.multiple_of(core * half + i * ROWS, ROWS), ROWS), :]
        for k in range(steps):
            logits = logit_ref[k, chunk(i), :]
            hits = ids == codes[:, k : k + 1]
            top = jnp.max(logits, axis=-1, keepdims=True)
            expo = jnp.exp(logits - top)
            total = jnp.sum(expo, axis=-1, keepdims=True)
            target = jnp.sum(jnp.where(hits, logits, 0.0), axis=-1, keepdims=True)
            expo_ref[k, chunk(i), :] = jnp.where(hits, 0.0, expo).astype(BF16)
            expo_ref[k, at_row(half, i), :] = jnp.where(hits, 1.0, 0.0).astype(BF16)
            for j, value in enumerate((top, total, target)):
                stats = jnp.where(spots == 3 * k + j, value, stats)
        stats_ref[chunk(i), :] = stats
        return carry

    lax.fori_loop(0, chunks, leave, 0)


def head_back_kernel(expo_ref, head_mine, head_pair, both_ref):
    vocab = head_mine.shape[2]
    for k in range(both_ref.shape[0]):
        both_ref[k] = dot_t(expo_ref[k, :, 0:vocab], head_mine[k]) + dot_t(
            expo_ref[k, :, vocab : 2 * vocab], head_pair[k]
        )


def mid_kernel(
    frames_total, both_ref, mid_ref, gain_ref, stats_ref, stats_side, out_ref,
    send_ref, keep_ref, sum_ref, loss_ref, low_ref,
):
    steps, half, _ = mid_ref.shape

    def leave(i, carry):
        mine = stats_ref[chunk(i), :]
        theirs = stats_side[chunk(i), :]
        spots = lax.broadcasted_iota(jnp.int32, (ROWS, steps), 1)
        losses = jnp.zeros((ROWS, steps), F32)
        added = 0.0
        for k in range(steps):
            top_a, sum_a, target_a = [mine[:, 3 * k + j : 3 * k + j + 1] for j in range(3)]
            top_b, sum_b, target_b = [theirs[:, 3 * k + j : 3 * k + j + 1] for j in range(3)]
            top = jnp.maximum(top_a, top_b)
            log_total = top + jnp.log(sum_a * jnp.exp(top_a - top) + sum_b * jnp.exp(top_b - top))
            target = target_a + target_b
            losses = jnp.where(spots == k, log_total - target, losses)
            part = both_ref[k, chunk(i), :] * (jnp.exp(top_a - log_total) / frames_total)
            hit = (jnp.exp(target - log_total) - 1.0) / frames_total
            part = part + both_ref[k, at_row(half, i), :] * hit
            grad = norm_back(mid_ref[k, chunk(i), :], gain_ref[...], part)
            low_ref[at_row(k * half, i), :] = grad.astype(BF16)
            added = added + grad
        sum_ref[chunk(i), :] = added
        loss_ref[chunk(i), :] = losses
        return carry

    lax.fori_loop(0, half // ROWS, leave, 0)
    middle = out_ref.shape[0] // 2
    send_ref[...] = dot_t(low_ref[...], out_ref[middle : 2 * middle, :]).astype(BF16)
    keep_ref[...] = dot_t(low_ref[...], out_ref[0:middle, :])


def attention_back_kernel(
    head_dim, keep_ref, recv_ref, proj_mine, proj_pair, soft_mine, soft_pair, qkv_mine, qkv_pair,
    stream_ref, gain_ref, sum_ref, part_ref, grad_ref, product_ref, prob_ref, back_mine, back_pair, normin_ref,
):
    steps, half, _ = stream_ref.shape
    lanes = keep_ref.shape[1] // 2
    chunks = half // ROWS
    pairs = pairs_of(steps)
    scale = head_dim ** (-0.5)
    ones = head_ones(lanes, head_dim)
    for j, (proj, soft, back) in enumerate(
        ((proj_mine, soft_mine, back_mine), (proj_pair, soft_pair, back_pair))
    ):
        span = slice(j * lanes, (j + 1) * lanes)

        def multiply(i, carry):
            rows = [at_row(k * half, i) for k in range(steps)]
            values = [proj[row, 2 * lanes : 3 * lanes] for row in rows]
            for a in range(steps):
                grad = (keep_ref[rows[a], span] + recv_ref[rows[a], span].astype(F32)).astype(BF16)
                grad_ref[rows[a], :] = grad
                for b in range(a + 1):
                    product_ref[at_row(pairs.index((a, b)) * half, i), :] = grad * values[b]
            return carry

        lax.fori_loop(0, chunks, multiply, 0)
        prob_ref[...] = dot(product_ref[...], ones)

        def spread(i, carry):
            rows = [at_row(k * half, i) for k in range(steps)]
            query_grad = [0.0] * steps
            key_grad = [0.0] * steps
            value_grad = [0.0] * steps
            for a in range(steps):
                first = pairs.index((a, 0))
                weights = [soft[at_row((first + b) * half, i), :] for b in range(a + 1)]
                probs = [prob_ref[at_row((first + b) * half, i), :] for b in range(a + 1)]
                inner = functools.reduce(jnp.add, [w * p for w, p in zip(weights, probs)])
                grad = grad_ref[rows[a], :].astype(F32)
                query = proj[rows[a], 0:lanes].astype(F32)
                for b in range(a + 1):
                    score = (weights[b] * (probs[b] - inner) * scale).astype(BF16).astype(F32)
                    key = proj[rows[b], lanes : 2 * lanes].astype(F32)
                    query_grad[a] = query_grad[a] + score * key
                    key_grad[b] = key_grad[b] + score * query
                    value_grad[b] = value_grad[b] + weights[b].astype(BF16).astype(F32) * grad
            for k in range(steps):
                back[rows[k], 0:lanes] = query_grad[k].astype(BF16)
                back[rows[k], lanes : 2 * lanes] = key_grad[k].astype(BF16)
                back[rows[k], 2 * lanes : 3 * lanes] = value_grad[k].astype(BF16)
            return carry

        lax.fori_loop(0, chunks, spread, 0)
    total = 0.0
    for back, weight in ((back_mine, qkv_mine), (back_pair, qkv_pair)):
        for part in range(3):
            total = total + dot_t(back[:, part * lanes : (part + 1) * lanes], weight[part])
    normin_ref[...] = total

    def leave(i, carry):
        part = sum_ref[chunk(i), :]
        for k in range(steps):
            part = part + norm_back(stream_ref[k, chunk(i), :], gain_ref[...], normin_ref[at_row(k * half, i), :])
        part_ref[chunk(i), :] = part.astype(BF16)
        return carry

    lax.fori_loop(0, chunks, leave, 0)


def sum_kernel(radix, low, part_ref, side_ref, grad_ref, *refs):
    outs, blocks_ref = refs[:radix], refs[radix]
    count, _, size = blocks_ref.shape
    digit = lax.axis_index("seq") // low % radix
    grad = (part_ref[...].astype(F32) + side_ref[...].astype(F32)).astype(BF16)
    grad_ref[...] = grad
    for j in range(count):
        blocks_ref[j] = grad[:, j * size : (j + 1) * size]
    for shift, out in enumerate(outs):
        for w in range(count // radix):
            out[0, w] = blocks_ref[w * radix + (digit + shift) % radix]


def pick_kernel(count, radix, low, *refs):
    digit = lax.axis_index("seq") // low % radix
    for shift, out in enumerate(refs[count:]):
        place = 0
        for item in refs[:count]:
            for q in range(item.shape[0]):
                for w in range(item.shape[1] // radix):
                    out[place, w] = item[q, w * radix + (digit + shift) % radix]
                place += 1


def hidden_grad_kernel(mine_ref, pair_ref, loss_mine, loss_pair, weight_ref, out_ref, loss_ref, full_ref):
    half = mine_ref.shape[0]
    core = lax.axis_index("tp") % 2
    low = pl.ds(pl.multiple_of(core * half, half), half)
    high = pl.ds(pl.multiple_of((1 - core) * half, half), half)
    full_ref[low, :] = mine_ref[...]
    full_ref[high, :] = pair_ref[...]
    loss_ref[low, :] = loss_mine[...]
    loss_ref[high, :] = loss_pair[...]
    out_ref[...] = dot_t(full_ref[...], weight_ref[...]).astype(BF16)


def project_kernel(count, *refs):
    states, mine, pair = refs[:count], refs[count : 2 * count], refs[2 * count : 3 * count]
    out_ref, grads_ref = refs[3 * count :]
    half = mine[0].shape[2]
    core = lax.axis_index("tp") % 2
    for p, (low, high) in enumerate(zip(mine, pair)):
        for q in range(low.shape[0]):
            base = 2 * q * half
            grads_ref[p, pl.ds(pl.multiple_of(base + core * half, half), half), :] = low[q, 0]
            grads_ref[p, pl.ds(pl.multiple_of(base + (1 - core) * half, half), half), :] = high[q, 0]
    total = 0.0
    for p, rows in enumerate(states):
        total = total + lax.dot_general(
            grads_ref[p], rows[...].reshape(-1, rows.shape[2]),
            (((0,), (0,)), ((), ())), preferred_element_type=F32,
        )
    out_ref[...] = total.T


def seq_radices(size):
    radices = []
    while size % 4 == 0:
        radices.append(4)
        size //= 4
    return [size] + radices if size > 1 else radices


def compute(hidden, w_proj, codes, embed_table, w_qkv, w_out, head_table, gain_attn, gain_head):
    frames, steps = codes.shape
    half = frames // 2
    width = w_proj.shape[1]
    head_dim = width // HEADS
    vocab_local = head_table.shape[2]
    lanes = w_qkv.shape[2]
    tp = lax.axis_size("tp")
    seq = lax.axis_size("seq")
    total = float(frames * seq * steps)
    pairs = len(pairs_of(steps))
    rows = steps * half
    gain_attn = gain_attn.reshape(1, width)
    gain_head = gain_head.reshape(1, width)

    def to_peer(value, flip):
        return lax.ppermute(value, "tp", [(i, i ^ flip) for i in range(tp)])

    def along(value, low, radix, shift):
        route = []
        for i in range(seq):
            digit = i // low % radix
            route.append((i, i + ((digit + shift) % radix - digit) * low))
        return lax.ppermute(value, "seq", route)

    cut = lanes // 2
    (out_part,) = call(cut_kernel, [((cut, width), BF16)], [], (w_out,), 6 * 10**9, limit=4)
    out_part = to_peer(out_part, 2)
    partial, partial_other = call(
        context_kernel, [((half, width), F32), ((half, width), BF16)], [],
        (hidden, w_proj), 6 * 10**9,
    )
    looked, looked_other = call(
        lookup_kernel,
        [((steps - 1, half, lanes), BF16)] * 2,
        [],
        (codes, embed_table), 2 * frames * embed_table.size,
    )
    partial = (partial + to_peer(partial_other, 1).astype(F32)).astype(BF16)
    partial_side = to_peer(partial, 2)
    looked = [looked, to_peer(looked_other, 1), to_peer(looked, 2), to_peer(looked_other, 3)]

    qkv_mine = w_qkv.transpose(1, 0, 2)
    qkv_pair = to_peer(qkv_mine, 1)
    head_pair = to_peer(head_table, 1)
    out_rest = along(out_part, 1, 2, 1)
    out_parts = (
        w_out, to_peer(w_out, 1), out_part, out_rest,
        to_peer(out_part, 1), to_peer(out_rest, 1),
    )
    states = [hidden[None]]
    low = 1
    for radix in seq_radices(seq):
        gathered = jnp.concatenate(states, axis=0)
        states = [gathered] + [along(gathered, low, radix, shift) for shift in range(1, radix)]
        low *= radix

    stream_in, att_mine, proj_mine, proj_pair, soft_mine, soft_pair = call(
        functools.partial(attention_kernel, head_dim),
        [((steps, half, width), F32), ((rows, 2 * lanes), BF16)]
        + [((rows, 3 * lanes), BF16)] * 2 + [((pairs * half, lanes), F32)] * 2,
        [
            pltpu.VMEM((steps - 1, half, width), BF16),
            pltpu.VMEM((rows, width), BF16),
            pltpu.VMEM((pairs * half, lanes), BF16),
            pltpu.VMEM((pairs * half, lanes), F32),
        ],
        (partial, partial_side, *looked, qkv_mine, qkv_pair, gain_attn), 4 * rows * qkv_mine.size,
    )
    att_theirs = to_peer(att_mine, 2)
    stream_mid, expo, stats, out_full = call(
        head_kernel,
        [((steps, half, width), F32), ((steps, 2 * half, 2 * vocab_local), BF16), ((half, 128), F32),
         ((tp * lanes, width), BF16)],
        [
            pltpu.VMEM((rows, width), F32),
            pltpu.VMEM((rows, width), BF16),
            pltpu.VMEM((steps, half, 2 * vocab_local), F32),
        ],
        (att_mine, att_theirs, *out_parts, stream_in, gain_head, codes, head_table, head_pair),
        4 * half * head_table.size + 2 * rows * width * width,
    )
    stats_side = to_peer(stats, 2)
    (both,) = call(
        head_back_kernel, [((steps, 2 * half, width), F32)], [],
        (expo, head_table, head_pair), 8 * half * head_table.size,
    )
    att_send, att_keep, mid_sum, losses = call(
        functools.partial(mid_kernel, total),
        [((rows, 2 * lanes), BF16), ((rows, 2 * lanes), F32), ((half, width), F32), ((half, steps), F32)],
        [pltpu.VMEM((rows, width), BF16)],
        (both, stream_mid, gain_head, stats, stats_side, out_full),
        2 * rows * width * width,
    )
    att_recv = to_peer(att_send, 2)
    (part,) = call(
        functools.partial(attention_back_kernel, head_dim),
        [((half, width), BF16)],
        [
            pltpu.VMEM((rows, lanes), BF16),
            pltpu.VMEM((pairs * half, lanes), BF16),
            pltpu.VMEM((pairs * half, lanes), F32),
            pltpu.VMEM((rows, 3 * lanes), BF16),
            pltpu.VMEM((rows, 3 * lanes), BF16),
            pltpu.VMEM((rows, width), F32),
        ],
        (att_keep, att_recv, proj_mine, proj_pair, soft_mine, soft_pair, qkv_mine, qkv_pair,
         stream_in, gain_attn, mid_sum),
        4 * rows * qkv_mine.size,
    )
    size = width // seq
    radices = seq_radices(seq)
    low, rest = 1, seq // radices[0]
    part_side = to_peer(part, 2)
    context_grad, *sends = call(
        functools.partial(sum_kernel, radices[0], 1),
        [((half, width), BF16)] + [((1, rest, half, size), BF16)] * radices[0],
        [pltpu.VMEM((seq, half, size), BF16)],
        (part, part_side), part.size, limit=4,
    )
    for stage, radix in enumerate(radices):
        if stage > 0:
            rest //= radix
            held = sum(item.shape[0] for item in owned)
            sends = call(
                functools.partial(pick_kernel, len(owned), radix, low),
                [((held, rest, half, size), BF16)] * radix, [], owned, part.size, limit=4,
            )
        owned = [sends[0]] + [along(item, low, radix, shift + 1) for shift, item in enumerate(sends[1:])]
        low *= radix
    grad_hidden, row_loss = call(
        hidden_grad_kernel,
        [((frames, w_proj.shape[0]), BF16), ((frames, steps), F32)],
        [pltpu.VMEM((frames, width), BF16)],
        (context_grad, to_peer(context_grad, 1), losses, to_peer(losses, 1), w_proj),
        2 * frames * w_proj.size,
    )
    paired = [to_peer(item, 1) for item in owned]
    held = states[0].shape[0]
    (grad_proj,) = call(
        functools.partial(project_kernel, len(states)),
        [((hidden.shape[1], size), F32)],
        [pltpu.VMEM((len(states), held * frames, size), BF16)],
        (*states, *owned, *paired), 2 * frames * seq * hidden.shape[1] * size, limit=40 if seq > 16 else 12,
    )
    return (row_loss, grad_hidden, grad_proj)


def solution(mesh):
    return jax.shard_map(
        compute,
        mesh=mesh,
        in_specs=(
            P("seq", "tp"),
            P("tp", None),
            P("seq", None),
            P(None, None, "tp"),
            P(None, None, "tp"),
            P("tp", None),
            P(None, None, "tp"),
            P(),
            P(),
        ),
        out_specs=(P("seq", None), P("seq", "tp"), P("tp", "seq")),
        check_vma=False,
    )
```

profile of v0, /device:TPU:0, one launch (start us, length us, event | category | flops | bytes accessed | tf_op | source)
XLA Modules:
  0.0 114.2 jit_solution(12373054149439036361)
XLA Ops:
  2.1 1.9 %copy-done.2 = bf16[3,2048,256]{2,1,0:T(8,128)(2,1)S(1)} copy-done((bf16[3,2048,256]{2,1,0:T(8,128)(2,1)S(1)}, bf16[3,2048,256]{2,1,0:T(8,128)(2,1)}, u32[]{:S(2)}) %copy-start.2) | copy-done | bytes 3145752
  5.2 2.8 %collective-permute-start.8 = (bf16[128,1024]{1,0:T(8,128)(2,1)S(1)}, bf16[128,1024]{1,0:T(8,128)(2,1)S(1)}, u32[]{:S(2)}, u32[]{:S(2)}) collective-permute-start(bf16[128,1024]{1,0:T(8,128)(2,1)S(1)} %shard_map.115), channel_id=1, source_target_pairs={{0,2},{1,3},{2,0},{3,1},{4,6},{5,7},{6,4},{7,5},{8,10},{9,11},{10,... | collective-permute-start | bytes 786440 | tf_op jit(solution)/shard_map/ppermute | solution.py:413
  8.5 2.0 %collective-permute-done.2.look1 = bf16[3,64,256]{2,1,0:T(8,128)(2,1)S(1)} collective-permute-done((bf16[3,64,256]{2,1,0:T(8,128)(2,1)S(1)}, bf16[3,64,256]{2,1,0:T(8,128)(2,1)S(1)}, u32[]{:S(2)}, u32[]{:S(2)}) %collective-permute-start.2) | collective-permute-done | bytes 98336 | tf_op jit(solution)/shard_map/ppermute | solution.py:413
  10.6 2.8 %collective-permute-start.3 = (bf16[3,64,256]{2,1,0:T(8,128)(2,1)S(1)}, bf16[3,64,256]{2,1,0:T(8,128)(2,1)S(1)}, u32[]{:S(2)}, u32[]{:S(2)}) collective-permute-start(bf16[3,64,256]{2,1,0:T(8,128)(2,1)S(1)} %get-tuple-element.32.look0), channel_id=1, source_target_pairs={{0,2},{1,3},{2,0},{3,1},{4,6},{5,7},{6,4},{7,5},{8,10},{9,11},{10,... | collective-permute-start | bytes 294920 | tf_op jit(solution)/shard_map/ppermute | solution.py:413
  13.4 3.4 %collective-permute-done.3.look2 = bf16[3,64,256]{2,1,0:T(8,128)(2,1)S(1)} collective-permute-done((bf16[3,64,256]{2,1,0:T(8,128)(2,1)S(1)}, bf16[3,64,256]{2,1,0:T(8,128)(2,1)S(1)}, u32[]{:S(2)}, u32[]{:S(2)}) %collective-permute-start.3) | collective-permute-done | bytes 98336 | tf_op jit(solution)/shard_map/ppermute | solution.py:413
  16.8 0.9 collective-permute-start.4
  17.8 0.9 collective-permute-start.7
  18.7 1.5 %collective-permute-start.9 = (bf16[128,1024]{1,0:T(8,128)(2,1)S(1)}, bf16[128,1024]{1,0:T(8,128)(2,1)S(1)}, u32[]{:S(2)}, u32[]{:S(2)}) collective-permute-start(bf16[128,1024]{1,0:T(8,128)(2,1)S(1)} %collective-permute-done.8.part_a), channel_id=1, source_target_pairs={{0,4},{4,0},{8,12},{12,8},{16,20},{20,16},{24,28},{28,24},{1,5},{5... | collective-permute-start | bytes 786440 | tf_op jit(solution)/shard_map/ppermute | solution.py:420
  20.2 1.4 %collective-permute-done.4.look3 = bf16[3,64,256]{2,1,0:T(8,128)(2,1)S(1)} collective-permute-done((bf16[3,64,256]{2,1,0:T(8,128)(2,1)S(1)}, bf16[3,64,256]{2,1,0:T(8,128)(2,1)S(1)}, u32[]{:S(2)}, u32[]{:S(2)}) %collective-permute-start.4) | collective-permute-done | bytes 98336 | tf_op jit(solution)/shard_map/ppermute | solution.py:413
  21.6 1.8 %collective-permute-start.1 = (bf16[64,1024]{1,0:T(8,128)(2,1)S(1)}, bf16[64,1024]{1,0:T(8,128)(2,1)S(1)}, u32[]{:S(2)}, u32[]{:S(2)}) collective-permute-start(bf16[64,1024]{1,0:T(8,128)(2,1)S(1)} %add_convert_fusion.own_ref), channel_id=1, source_target_pairs={{0,2},{1,3},{2,0},{3,1},{4,6},{5,7},{6,4},{7,5},{8,10},{9,11},{10,... | collective-permute-start | bytes 393224 | tf_op jit(solution)/shard_map/ppermute | solution.py:413
  23.4 3.7 %collective-permute-done.1.side_ref = bf16[64,1024]{1,0:T(8,128)(2,1)S(1)} collective-permute-done((bf16[64,1024]{1,0:T(8,128)(2,1)S(1)}, bf16[64,1024]{1,0:T(8,128)(2,1)S(1)}, u32[]{:S(2)}, u32[]{:S(2)}) %collective-permute-start.1) | collective-permute-done | bytes 131104 | tf_op jit(solution)/shard_map/ppermute | solution.py:413
  27.7 3.3 %shard_map.114 = (f32[4,64,1024]{2,1,0:T(8,128)S(1)}, bf16[256,512]{1,0:T(8,128)(2,1)S(1)}, bf16[256,768]{1,0:T(8,128)(2,1)S(1)}, bf16[256,768]{1,0:T(8,128)(2,1...) custom-call(bf16[64,1024]{1,0:T(8,128)(2,1)S(1)} %add_convert_fusion.own_ref, ...), custom_call_target="tpu_custom_call" | custom-call | flops 805306368 | bytes 2684354 | tf_op jit(solution)/shard_map/pallas_call | solution.py:51
  31.0 1.6 %collective-permute-start.6 = (bf16[256,512]{1,0:T(8,128)(2,1)S(1)}, bf16[256,512]{1,0:T(8,128)(2,1)S(1)}, u32[]{:S(2)}, u32[]{:S(2)}) collective-permute-start(bf16[256,512]{1,0:T(8,128)(2,1)S(1)} %get-tuple-element.34.att_mine), channel_id=1, source_target_pairs={{0,2},{1,3},{2,0},{3,1},{4,6},{5,7},{6,4},{7,5},{8,10},{9,11},{10,... | collective-permute-start | bytes 786440 | tf_op jit(solution)/shard_map/ppermute | solution.py:413
  32.6 1.5 %collective-permute-start.18 = (bf16[1,128,1024]{2,1,0:T(8,128)(2,1)S(1)}, bf16[1,128,1024]{2,1,0:T(8,128)(2,1)S(1)}, u32[]{:S(2)}, u32[]{:S(2)}) collective-permute-start(bf16[1,128,1024]{2,1,0:T(8,128)(2,1)S(1)} %bitcast.7), channel_id=1, source_target_pairs={{0,4},{4,0},{8,12},{12,8},{16,20},{20,16},{24,28},{28,24},{1,5},{5... | collective-permute-start | bytes 786440 | tf_op jit(solution)/shard_map/ppermute | solution.py:420
  34.1 5.1 %collective-permute-done.6.att_theirs = bf16[256,512]{1,0:T(8,128)(2,1)S(1)} collective-permute-done((bf16[256,512]{1,0:T(8,128)(2,1)S(1)}, bf16[256,512]{1,0:T(8,128)(2,1)S(1)}, u32[]{:S(2)}, u32[]{:S(2)}) %collective-permute-start.6) | collective-permute-done | bytes 262176 | tf_op jit(solution)/shard_map/ppermute | solution.py:413
  39.3 6.2 %shard_map.116 = (f32[4,64,1024]{2,1,0:T(8,128)S(1)}, bf16[4,128,1024]{2,1,0:T(8,128)(2,1)S(1)}, f32[64,128]{1,0:T(8,128)S(1)}, bf16[1024,1024]{1,0:T(8,128)(2,1)S(1)}) custom-call(bf16[256,512]{1,0:T(8,128)(2,1)S(1)} %get-tuple-element.34.att_mine, bf16[256,512]{1,0:T(8,128)(2,1)S(1)} %collective-permute-done.6.att_theirs, bf16[256,1024]{1,0:T(8,128)(2,1)S(1)} %copy-done.4, ...), custom_call_target="tpu_custom_call" | custom-call | flops 1073741824 | bytes 3579139 | tf_op jit(solution)/shard_map/pallas_call | solution.py:51
  45.4 1.6 %collective-permute-start.13 = (f32[64,128]{1,0:T(8,128)S(1)}, f32[64,128]{1,0:T(8,128)S(1)}, u32[]{:S(2)}, u32[]{:S(2)}) collective-permute-start(f32[64,128]{1,0:T(8,128)S(1)} %get-tuple-element.38.stats_ref), channel_id=1, source_target_pairs={{0,2},{1,3},{2,0},{3,1},{4,6},{5,7},{6,4},{7,5},{8,10},{9,11},{10,... | collective-permute-start | bytes 98312 | tf_op jit(solution)/shard_map/ppermute | solution.py:413
  47.1 5.0 %shard_map.117.both_ref = f32[4,128,1024]{2,1,0:T(8,128)S(1)} custom-call(bf16[4,128,1024]{2,1,0:T(8,128)(2,1)S(1)} %get-tuple-element.36.expo_ref, bf16[4,1024,512]{2,1,0:T(8,128)(2,1)S(1)} %copy-done, bf16[4,1024,512]{2,1,0:T(8,128)(2,1)} %collective-permute-done.12.head_pair), custom_call_target="tpu_custom_call" | custom-call | flops 1073741824 | bytes 3579139 | tf_op jit(solution)/shard_map/pallas_call | solution.py:51
  52.1 2.6 %shard_map.118 = (bf16[256,512]{1,0:T(8,128)(2,1)S(1)}, f32[256,512]{1,0:T(8,128)S(1)}, f32[64,1024]{1,0:T(8,128)S(1)}, f32[64,4]{1,0:T(8,128)S(1)}) custom-call(f32[4,128,1024]{2,1,0:T(8,128)S(1)} %shard_map.117.both_ref, f32[4,64,1024]{2,1,0:T(8,128)S(1)} %get-tuple-element.37.mid_ref, f32[1,1024]{1,0:T(1,128)S(1)} %bitcast.10, ...), custom_call_target="tpu_custom_call" | custom-call | flops 536870912 | bytes 1789569 | tf_op jit(solution)/shard_map/pallas_call | solution.py:51
  55.2 2.1 %collective-permute-start.19 = (bf16[2,128,1024]{2,1,0:T(8,128)(2,1)S(1)}, bf16[2,128,1024]{2,1,0:T(8,128)(2,1)S(1)}, u32[]{:S(2)}, u32[]{:S(2)}) collective-permute-start(bf16[2,128,1024]{2,1,0:T(8,128)(2,1)S(1)} %pad_maximum_fusion.refs_0_), channel_id=1, source_target_pairs={{0,8},{4,12},{8,16},{12,20},{16,24},{20,28},{24,0},{28,4},{1,9},{5... | collective-permute-start | bytes 1572872 | tf_op jit(solution)/shard_map/ppermute | solution.py:420
  57.4 2.6 %collective-permute-start.20 = (bf16[2,128,1024]{2,1,0:T(8,128)(2,1)S(1)}, bf16[2,128,1024]{2,1,0:T(8,128)(2,1)S(1)}, u32[]{:S(2)}, u32[]{:S(2)}) collective-permute-start(bf16[2,128,1024]{2,1,0:T(8,128)(2,1)S(1)} %pad_maximum_fusion.refs_0_), channel_id=1, source_target_pairs={{0,16},{4,20},{8,24},{12,28},{16,0},{20,4},{24,8},{28,12},{1,17},{... | collective-permute-start | bytes 1572872 | tf_op jit(solution)/shard_map/ppermute | solution.py:420
  60.0 1.4 %collective-permute-start.21 = (bf16[2,128,1024]{2,1,0:T(8,128)(2,1)S(1)}, bf16[2,128,1024]{2,1,0:T(8,128)(2,1)}, u32[]{:S(2)}, u32[]{:S(2)}) collective-permute-start(bf16[2,128,1024]{2,1,0:T(8,128)(2,1)S(1)} %pad_maximum_fusion.refs_0_), channel_id=1, source_target_pairs={{0,24},{4,28},{8,0},{12,4},{16,8},{20,12},{24,16},{28,20},{1,25},{... | collective-permute-start | bytes 1572872 | tf_op jit(solution)/shard_map/ppermute | solution.py:420
  61.8 3.1 %shard_map.119.part_ref = bf16[64,1024]{1,0:T(8,128)(2,1)S(1)} custom-call(f32[256,512]{1,0:T(8,128)S(1)} %get-tuple-element.40.keep_ref, bf16[256,512]{1,0:T(8,128)(2,1)S(1)} %collective-permute-done.14.recv_ref, bf16[256,768]{1,0:T(8,128)(2,1)S(1)} %get-tuple-element.42.proj_mine, bf16[256,768]{1,0:T(8,128)(2,1)S(1)} %get-tuple-element.43.proj_pair, ...), custom_call_target="tpu_custom_call" | custom-call | flops 805306368 | bytes 2684354 | tf_op jit(solution)/shard_map/pallas_call | solution.py:51
  65.6 4.4 %collective-permute-done.15.side_ref = bf16[64,1024]{1,0:T(8,128)(2,1)S(1)} collective-permute-done((bf16[64,1024]{1,0:T(8,128)(2,1)S(1)}, bf16[64,1024]{1,0:T(8,128)(2,1)S(1)}, u32[]{:S(2)}, u32[]{:S(2)}) %collective-permute-start.15) | collective-permute-done | bytes 131104 | tf_op jit(solution)/shard_map/ppermute | solution.py:413
  70.2 1.6 %collective-permute-start.22 = (bf16[1,4,64,128]{3,2,1,0:T(8,128)(2,1)S(1)}, bf16[1,4,64,128]{3,2,1,0:T(8,128)(2,1)S(1)}, u32[]{:S(2)}, u32[]{:S(2)}) collective-permute-start(bf16[1,4,64,128]{3,2,1,0:T(8,128)(2,1)S(1)} %get-tuple-element.52), channel_id=1, source_target_pairs={{0,4},{4,0},{8,12},{12,8},{16,20},{20,16},{24,28},{28,24},{1,5},{5... | collective-permute-start | bytes 196616 | tf_op jit(solution)/shard_map/ppermute | solution.py:420
  71.7 2.9 %collective-permute-done.22.refs_1_ = bf16[1,4,64,128]{3,2,1,0:T(8,128)(2,1)S(1)} collective-permute-done((bf16[1,4,64,128]{3,2,1,0:T(8,128)(2,1)S(1)}, bf16[1,4,64,128]{3,2,1,0:T(8,128)(2,1)S(1)}, u32[]{:S(2)}, u32[]{:S(2)}) %collective-permute-start.22) | collective-permute-done | bytes 65568 | tf_op jit(solution)/shard_map/ppermute | solution.py:420
  74.7 19.1 %collective-permute-start.23 = (bf16[2,1,64,128]{3,2,1,0:T(8,128)(2,1)S(1)}, bf16[2,1,64,128]{3,2,1,0:T(8,128)(2,1)S(1)}, u32[]{:S(2)}, u32[]{:S(2)}) collective-permute-start(bf16[2,1,64,128]{3,2,1,0:T(8,128)(2,1)S(1)} %get-tuple-element.54), channel_id=1, source_target_pairs={{0,8},{4,12},{8,16},{12,20},{16,24},{20,28},{24,0},{28,4},{1,9},{5... | collective-permute-start | bytes 98312 | tf_op jit(solution)/shard_map/ppermute | solution.py:420
  93.7 1.9 %collective-permute-start.24 = (bf16[2,1,64,128]{3,2,1,0:T(8,128)(2,1)S(1)}, bf16[2,1,64,128]{3,2,1,0:T(8,128)(2,1)S(1)}, u32[]{:S(2)}, u32[]{:S(2)}) collective-permute-start(bf16[2,1,64,128]{3,2,1,0:T(8,128)(2,1)S(1)} %get-tuple-element.55), channel_id=1, source_target_pairs={{0,16},{4,20},{8,24},{12,28},{16,0},{20,4},{24,8},{28,12},{1,17},{... | collective-permute-start | bytes 98312 | tf_op jit(solution)/shard_map/ppermute | solution.py:420
  95.7 10.9 %collective-permute-start.25 = (bf16[2,1,64,128]{3,2,1,0:T(8,128)(2,1)S(1)}, bf16[2,1,64,128]{3,2,1,0:T(8,128)(2,1)S(1)}, u32[]{:S(2)}, u32[]{:S(2)}) collective-permute-start(bf16[2,1,64,128]{3,2,1,0:T(8,128)(2,1)S(1)} %get-tuple-element.56), channel_id=1, source_target_pairs={{0,24},{4,28},{8,0},{12,4},{16,8},{20,12},{24,16},{28,20},{1,25},{... | collective-permute-start | bytes 98312 | tf_op jit(solution)/shard_map/ppermute | solution.py:420
  107.0 1.9 %collective-permute-done.25.refs_7_ = bf16[2,1,64,128]{3,2,1,0:T(8,128)(2,1)S(1)} collective-permute-done((bf16[2,1,64,128]{3,2,1,0:T(8,128)(2,1)S(1)}, bf16[2,1,64,128]{3,2,1,0:T(8,128)(2,1)S(1)}, u32[]{:S(2)}, u32[]{:S(2)}) %collective-permute-start.25) | collective-permute-done | bytes 32800 | tf_op jit(solution)/shard_map/ppermute | solution.py:420
  109.5 1.5 %shard_map.121 = (bf16[128,1024]{1,0:T(8,128)(2,1)}, f32[128,4]{1,0:T(8,128)S(1)}) custom-call(bf16[64,1024]{1,0:T(8,128)(2,1)S(1)} %get-tuple-element.47.mine_ref, bf16[64,1024]{1,0:T(8,128)(2,1)S(1)} %collective-permute-done.16.pair_ref, f32[64,4]{1,0:T(8,128)S(1)} %get-tuple-element.48.loss_mine, f32[64,4]{1,0:T(8,128)S(1)} %collective-permute-done.17.loss_pair, ...), custom_call_target="tpu_custom_call" | custom-call | flops 268435456 | bytes 894784 | tf_op jit(solution)/shard_map/pallas_call | solution.py:51
  111.7 2.5 %shard_map.123 = f32[1024,128]{1,0:T(8,128)} custom-call(bf16[2,128,1024]{2,1,0:T(8,128)(2,1)S(1)} %pad_maximum_fusion.refs_0_, bf16[2,128,1024]{2,1,0:T(8,128)(2,1)S(1)} %collective-permute-done.19.refs_1_, bf16[2,128,1024]{2,1,0:T(8,128)(2,1)S(1)} %collective-permute-done.20.refs_2_, bf16[2,128,1024]{2,1,0:T(8,128)(2,1)} %collective-permute-done.21.refs_3_, ...), custom_call_target="tpu_custom_call" | custom-call | flops 268435456 | bytes 894784 | tf_op jit(solution)/shard_map/pallas_call | solution.py:51
  (60 shorter events, 7.3 us)
Async XLA Ops:
  0.6 38.6 %collective-permute-start.12 = (bf16[4,1024,512]{2,1,0:T(8,128)(2,1)}, bf16[4,1024,512]{2,1,0:T(8,128)(2,1)}, u32[]{:S(2)}, u32[]{:S(2)}) collective-permute-start(bf16[4,1024,512]{2,1,0:T(8,128)(2,1)} %head_mine.3), channel_id=1, source_target_pairs={{0,1},{1,0},{2,3},{3,2},{4,5},{5,4},{6,7},{7,6},{8,9},{9,8},{10,11... | collective-permute-start | bytes 12582920 | tf_op jit(solution)/shard_map/ppermute | solution.py:413
  1.2 26.5 %collective-permute-start.5 = (bf16[3,1024,256]{2,1,0:T(8,128)(2,1)}, bf16[3,1024,256]{2,1,0:T(8,128)(2,1)S(1)}, u32[]{:S(2)}, u32[]{:S(2)}) collective-permute-start(bf16[3,1024,256]{2,1,0:T(8,128)(2,1)} %bitcast.4), channel_id=1, source_target_pairs={{0,1},{1,0},{2,3},{3,2},{4,5},{5,4},{6,7},{7,6},{8,9},{9,8},{10,11... | collective-permute-start | bytes 4718600 | tf_op jit(solution)/shard_map/ppermute | solution.py:413
  4.7 5.9 %collective-permute-start.2 = (bf16[3,64,256]{2,1,0:T(8,128)(2,1)S(1)}, bf16[3,64,256]{2,1,0:T(8,128)(2,1)S(1)}, u32[]{:S(2)}, u32[]{:S(2)}) collective-permute-start(bf16[3,64,256]{2,1,0:T(8,128)(2,1)S(1)} %get-tuple-element.33), channel_id=1, source_target_pairs={{0,1},{1,0},{2,3},{3,2},{4,5},{5,4},{6,7},{7,6},{8,9},{9,8},{10,11... | collective-permute-start | bytes 294920 | tf_op jit(solution)/shard_map/ppermute | solution.py:413
  5.2 22.5 %copy-start.1 = (bf16[1024,3,256]{2,0,1:T(8,128)(2,1)S(1)}, bf16[1024,3,256]{2,0,1:T(8,128)(2,1)}, u32[]{:S(2)}) copy-start(bf16[1024,3,256]{2,0,1:T(8,128)(2,1)} %param.13) | copy-start | bytes 4718596
  5.2 22.5 %copy-start.7 = (f32[1024]{0:T(1024)S(1)}, f32[1024]{0:T(1024)}, u32[]{:S(2)}) copy-start(f32[1024]{0:T(1024)} %param.16) | copy-start | bytes 12292
  5.2 13.5 %collective-permute-start.8 = (bf16[128,1024]{1,0:T(8,128)(2,1)S(1)}, bf16[128,1024]{1,0:T(8,128)(2,1)S(1)}, u32[]{:S(2)}, u32[]{:S(2)}) collective-permute-start(bf16[128,1024]{1,0:T(8,128)(2,1)S(1)} %shard_map.115), channel_id=1, source_target_pairs={{0,2},{1,3},{2,0},{3,1},{4,6},{5,7},{6,4},{7,5},{8,10},{9,11},{10,... | collective-permute-start | bytes 786440 | tf_op jit(solution)/shard_map/ppermute | solution.py:413
  8.5 9.3 %collective-permute-start = (bf16[64,1024]{1,0:T(8,128)(2,1)S(1)}, bf16[64,1024]{1,0:T(8,128)(2,1)S(1)}, u32[]{:S(2)}, u32[]{:S(2)}) collective-permute-start(bf16[64,1024]{1,0:T(8,128)(2,1)S(1)} %get-tuple-element.31), channel_id=1, source_target_pairs={{0,1},{1,0},{2,3},{3,2},{4,5},{5,4},{6,7},{7,6},{8,9},{9,8},{10,11... | collective-permute-start | bytes 393224 | tf_op jit(solution)/shard_map/ppermute | solution.py:413
  10.6 6.3 %collective-permute-start.3 = (bf16[3,64,256]{2,1,0:T(8,128)(2,1)S(1)}, bf16[3,64,256]{2,1,0:T(8,128)(2,1)S(1)}, u32[]{:S(2)}, u32[]{:S(2)}) collective-permute-start(bf16[3,64,256]{2,1,0:T(8,128)(2,1)S(1)} %get-tuple-element.32.look0), channel_id=1, source_target_pairs={{0,2},{1,3},{2,0},{3,1},{4,6},{5,7},{6,4},{7,5},{8,10},{9,11},{10,... | collective-permute-start | bytes 294920 | tf_op jit(solution)/shard_map/ppermute | solution.py:413
  16.8 4.8 %collective-permute-start.4 = (bf16[3,64,256]{2,1,0:T(8,128)(2,1)S(1)}, bf16[3,64,256]{2,1,0:T(8,128)(2,1)S(1)}, u32[]{:S(2)}, u32[]{:S(2)}) collective-permute-start(bf16[3,64,256]{2,1,0:T(8,128)(2,1)S(1)} %get-tuple-element.33), channel_id=1, source_target_pairs={{0,3},{1,2},{2,1},{3,0},{4,7},{5,6},{6,5},{7,4},{8,11},{9,10},{10,... | collective-permute-start | bytes 294920 | tf_op jit(solution)/shard_map/ppermute | solution.py:413
  17.8 16.3 %collective-permute-start.7 = (bf16[256,1024]{1,0:T(8,128)(2,1)S(1)}, bf16[256,1024]{1,0:T(8,128)(2,1)S(1)}, u32[]{:S(2)}, u32[]{:S(2)}) collective-permute-start(bf16[256,1024]{1,0:T(8,128)(2,1)S(1)} %copy-done.4), channel_id=1, source_target_pairs={{0,1},{1,0},{2,3},{3,2},{4,5},{5,4},{6,7},{7,6},{8,9},{9,8},{10,11... | collective-permute-start | bytes 1572872 | tf_op jit(solution)/shard_map/ppermute | solution.py:413
  18.7 8.5 %collective-permute-start.9 = (bf16[128,1024]{1,0:T(8,128)(2,1)S(1)}, bf16[128,1024]{1,0:T(8,128)(2,1)S(1)}, u32[]{:S(2)}, u32[]{:S(2)}) collective-permute-start(bf16[128,1024]{1,0:T(8,128)(2,1)S(1)} %collective-permute-done.8.part_a), channel_id=1, source_target_pairs={{0,4},{4,0},{8,12},{12,8},{16,20},{20,16},{24,28},{28,24},{1,5},{5... | collective-permute-start | bytes 786440 | tf_op jit(solution)/shard_map/ppermute | solution.py:420
  21.6 5.5 %collective-permute-start.1 = (bf16[64,1024]{1,0:T(8,128)(2,1)S(1)}, bf16[64,1024]{1,0:T(8,128)(2,1)S(1)}, u32[]{:S(2)}, u32[]{:S(2)}) collective-permute-start(bf16[64,1024]{1,0:T(8,128)(2,1)S(1)} %add_convert_fusion.own_ref), channel_id=1, source_target_pairs={{0,2},{1,3},{2,0},{3,1},{4,6},{5,7},{6,4},{7,5},{8,10},{9,11},{10,... | collective-permute-start | bytes 393224 | tf_op jit(solution)/shard_map/ppermute | solution.py:413
  27.2 5.4 %collective-permute-start.10 = (bf16[128,1024]{1,0:T(8,128)(2,1)S(1)}, bf16[128,1024]{1,0:T(8,128)(2,1)S(1)}, u32[]{:S(2)}, u32[]{:S(2)}) collective-permute-start(bf16[128,1024]{1,0:T(8,128)(2,1)S(1)} %collective-permute-done.8.part_a), channel_id=1, source_target_pairs={{0,1},{1,0},{2,3},{3,2},{4,5},{5,4},{6,7},{7,6},{8,9},{9,8},{10,11... | collective-permute-start | bytes 786440 | tf_op jit(solution)/shard_map/ppermute | solution.py:413
  27.2 7.0 %collective-permute-start.11 = (bf16[128,1024]{1,0:T(8,128)(2,1)S(1)}, bf16[128,1024]{1,0:T(8,128)(2,1)S(1)}, u32[]{:S(2)}, u32[]{:S(2)}) collective-permute-start(bf16[128,1024]{1,0:T(8,128)(2,1)S(1)} %collective-permute-done.9.part_b), channel_id=1, source_target_pairs={{0,1},{1,0},{2,3},{3,2},{4,5},{5,4},{6,7},{7,6},{8,9},{9,8},{10,11... | collective-permute-start | bytes 786440 | tf_op jit(solution)/shard_map/ppermute | solution.py:413
  31.0 8.3 %collective-permute-start.6 = (bf16[256,512]{1,0:T(8,128)(2,1)S(1)}, bf16[256,512]{1,0:T(8,128)(2,1)S(1)}, u32[]{:S(2)}, u32[]{:S(2)}) collective-permute-start(bf16[256,512]{1,0:T(8,128)(2,1)S(1)} %get-tuple-element.34.att_mine), channel_id=1, source_target_pairs={{0,2},{1,3},{2,0},{3,1},{4,6},{5,7},{6,4},{7,5},{8,10},{9,11},{10,... | collective-permute-start | bytes 786440 | tf_op jit(solution)/shard_map/ppermute | solution.py:413
  32.6 22.6 %collective-permute-start.18 = (bf16[1,128,1024]{2,1,0:T(8,128)(2,1)S(1)}, bf16[1,128,1024]{2,1,0:T(8,128)(2,1)S(1)}, u32[]{:S(2)}, u32[]{:S(2)}) collective-permute-start(bf16[1,128,1024]{2,1,0:T(8,128)(2,1)S(1)} %bitcast.7), channel_id=1, source_target_pairs={{0,4},{4,0},{8,12},{12,8},{16,20},{20,16},{24,28},{28,24},{1,5},{5... | collective-permute-start | bytes 786440 | tf_op jit(solution)/shard_map/ppermute | solution.py:420
  45.4 6.6 %collective-permute-start.13 = (f32[64,128]{1,0:T(8,128)S(1)}, f32[64,128]{1,0:T(8,128)S(1)}, u32[]{:S(2)}, u32[]{:S(2)}) collective-permute-start(f32[64,128]{1,0:T(8,128)S(1)} %get-tuple-element.38.stats_ref), channel_id=1, source_target_pairs={{0,2},{1,3},{2,0},{3,1},{4,6},{5,7},{6,4},{7,5},{8,10},{9,11},{10,... | collective-permute-start | bytes 98312 | tf_op jit(solution)/shard_map/ppermute | solution.py:413
  54.7 7.2 %collective-permute-start.14 = (bf16[256,512]{1,0:T(8,128)(2,1)S(1)}, bf16[256,512]{1,0:T(8,128)(2,1)S(1)}, u32[]{:S(2)}, u32[]{:S(2)}) collective-permute-start(bf16[256,512]{1,0:T(8,128)(2,1)S(1)} %get-tuple-element.41), channel_id=1, source_target_pairs={{0,2},{1,3},{2,0},{3,1},{4,6},{5,7},{6,4},{7,5},{8,10},{9,11},{10,... | collective-permute-start | bytes 786440 | tf_op jit(solution)/shard_map/ppermute | solution.py:413
  55.2 19.4 %collective-permute-start.19 = (bf16[2,128,1024]{2,1,0:T(8,128)(2,1)S(1)}, bf16[2,128,1024]{2,1,0:T(8,128)(2,1)S(1)}, u32[]{:S(2)}, u32[]{:S(2)}) collective-permute-start(bf16[2,128,1024]{2,1,0:T(8,128)(2,1)S(1)} %pad_maximum_fusion.refs_0_), channel_id=1, source_target_pairs={{0,8},{4,12},{8,16},{12,20},{16,24},{20,28},{24,0},{28,4},{1,9},{5... | collective-permute-start | bytes 1572872 | tf_op jit(solution)/shard_map/ppermute | solution.py:420
  57.4 36.4 %collective-permute-start.20 = (bf16[2,128,1024]{2,1,0:T(8,128)(2,1)S(1)}, bf16[2,128,1024]{2,1,0:T(8,128)(2,1)S(1)}, u32[]{:S(2)}, u32[]{:S(2)}) collective-permute-start(bf16[2,128,1024]{2,1,0:T(8,128)(2,1)S(1)} %pad_maximum_fusion.refs_0_), channel_id=1, source_target_pairs={{0,16},{4,20},{8,24},{12,28},{16,0},{20,4},{24,8},{28,12},{1,17},{... | collective-permute-start | bytes 1572872 | tf_op jit(solution)/shard_map/ppermute | solution.py:420
  60.0 51.7 %collective-permute-start.21 = (bf16[2,128,1024]{2,1,0:T(8,128)(2,1)S(1)}, bf16[2,128,1024]{2,1,0:T(8,128)(2,1)}, u32[]{:S(2)}, u32[]{:S(2)}) collective-permute-start(bf16[2,128,1024]{2,1,0:T(8,128)(2,1)S(1)} %pad_maximum_fusion.refs_0_), channel_id=1, source_target_pairs={{0,24},{4,28},{8,0},{12,4},{16,8},{20,12},{24,16},{28,20},{1,25},{... | collective-permute-start | bytes 1572872 | tf_op jit(solution)/shard_map/ppermute | solution.py:420
  65.0 5.0 %collective-permute-start.15 = (bf16[64,1024]{1,0:T(8,128)(2,1)S(1)}, bf16[64,1024]{1,0:T(8,128)(2,1)S(1)}, u32[]{:S(2)}, u32[]{:S(2)}) collective-permute-start(bf16[64,1024]{1,0:T(8,128)(2,1)S(1)} %shard_map.119.part_ref), channel_id=1, source_target_pairs={{0,2},{1,3},{2,0},{3,1},{4,6},{5,7},{6,4},{7,5},{8,10},{9,11},{10,... | collective-permute-start | bytes 393224 | tf_op jit(solution)/shard_map/ppermute | solution.py:413
  70.1 38.9 %collective-permute-start.16 = (bf16[64,1024]{1,0:T(8,128)(2,1)S(1)}, bf16[64,1024]{1,0:T(8,128)(2,1)S(1)}, u32[]{:S(2)}, u32[]{:S(2)}) collective-permute-start(bf16[64,1024]{1,0:T(8,128)(2,1)S(1)} %get-tuple-element.47.mine_ref), channel_id=1, source_target_pairs={{0,1},{1,0},{2,3},{3,2},{4,5},{5,4},{6,7},{7,6},{8,9},{9,8},{10,11... | collective-permute-start | bytes 393224 | tf_op jit(solution)/shard_map/ppermute | solution.py:413
  70.2 4.5 %collective-permute-start.22 = (bf16[1,4,64,128]{3,2,1,0:T(8,128)(2,1)S(1)}, bf16[1,4,64,128]{3,2,1,0:T(8,128)(2,1)S(1)}, u32[]{:S(2)}, u32[]{:S(2)}) collective-permute-start(bf16[1,4,64,128]{3,2,1,0:T(8,128)(2,1)S(1)} %get-tuple-element.52), channel_id=1, source_target_pairs={{0,4},{4,0},{8,12},{12,8},{16,20},{20,16},{24,28},{28,24},{1,5},{5... | collective-permute-start | bytes 196616 | tf_op jit(solution)/shard_map/ppermute | solution.py:420
  74.7 21.0 %collective-permute-start.17 = (f32[64,4]{1,0:T(8,128)S(1)}, f32[64,4]{1,0:T(8,128)S(1)}, u32[]{:S(2)}, u32[]{:S(2)}) collective-permute-start(f32[64,4]{1,0:T(8,128)S(1)} %get-tuple-element.48.loss_mine), channel_id=1, source_target_pairs={{0,1},{1,0},{2,3},{3,2},{4,5},{5,4},{6,7},{7,6},{8,9},{9,8},{10,11... | collective-permute-start | bytes 3080 | tf_op jit(solution)/shard_map/ppermute | solution.py:413
  74.7 31.8 %collective-permute-start.23 = (bf16[2,1,64,128]{3,2,1,0:T(8,128)(2,1)S(1)}, bf16[2,1,64,128]{3,2,1,0:T(8,128)(2,1)S(1)}, u32[]{:S(2)}, u32[]{:S(2)}) collective-permute-start(bf16[2,1,64,128]{3,2,1,0:T(8,128)(2,1)S(1)} %get-tuple-element.54), channel_id=1, source_target_pairs={{0,8},{4,12},{8,16},{12,20},{16,24},{20,28},{24,0},{28,4},{1,9},{5... | collective-permute-start | bytes 98312 | tf_op jit(solution)/shard_map/ppermute | solution.py:420
  93.7 12.8 %collective-permute-start.24 = (bf16[2,1,64,128]{3,2,1,0:T(8,128)(2,1)S(1)}, bf16[2,1,64,128]{3,2,1,0:T(8,128)(2,1)S(1)}, u32[]{:S(2)}, u32[]{:S(2)}) collective-permute-start(bf16[2,1,64,128]{3,2,1,0:T(8,128)(2,1)S(1)} %get-tuple-element.55), channel_id=1, source_target_pairs={{0,16},{4,20},{8,24},{12,28},{16,0},{20,4},{24,8},{28,12},{1,17},{... | collective-permute-start | bytes 98312 | tf_op jit(solution)/shard_map/ppermute | solution.py:420
  95.7 13.3 %collective-permute-start.25 = (bf16[2,1,64,128]{3,2,1,0:T(8,128)(2,1)S(1)}, bf16[2,1,64,128]{3,2,1,0:T(8,128)(2,1)S(1)}, u32[]{:S(2)}, u32[]{:S(2)}) collective-permute-start(bf16[2,1,64,128]{3,2,1,0:T(8,128)(2,1)S(1)} %get-tuple-element.56), channel_id=1, source_target_pairs={{0,24},{4,28},{8,0},{12,4},{16,8},{20,12},{24,16},{28,20},{1,25},{... | collective-permute-start | bytes 98312 | tf_op jit(solution)/shard_map/ppermute | solution.py:420
  106.5 5.1 %collective-permute-start.26 = (bf16[2,1,64,128]{3,2,1,0:T(8,128)(2,1)S(1)}, bf16[2,1,64,128]{3,2,1,0:T(8,128)(2,1)S(1)}, u32[]{:S(2)}, u32[]{:S(2)}) collective-permute-start(bf16[2,1,64,128]{3,2,1,0:T(8,128)(2,1)S(1)} %get-tuple-element.53.refs_4_), channel_id=1, source_target_pairs={{0,1},{1,0},{2,3},{3,2},{4,5},{5,4},{6,7},{7,6},{8,9},{9,8},{10,11... | collective-permute-start | bytes 98312 | tf_op jit(solution)/shard_map/ppermute | solution.py:413
  106.5 5.1 %collective-permute-start.27 = (bf16[2,1,64,128]{3,2,1,0:T(8,128)(2,1)S(1)}, bf16[2,1,64,128]{3,2,1,0:T(8,128)(2,1)S(1)}, u32[]{:S(2)}, u32[]{:S(2)}) collective-permute-start(bf16[2,1,64,128]{3,2,1,0:T(8,128)(2,1)S(1)} %collective-permute-done.23.refs_5_), channel_id=1, source_target_pairs={{0,1},{1,0},{2,3},{3,2},{4,5},{5,4},{6,7},{7,6},{8,9},{9,8},{10,11... | collective-permute-start | bytes 98312 | tf_op jit(solution)/shard_map/ppermute | solution.py:413
  109.0 2.7 %collective-permute-start.28 = (bf16[2,1,64,128]{3,2,1,0:T(8,128)(2,1)S(1)}, bf16[2,1,64,128]{3,2,1,0:T(8,128)(2,1)S(1)}, u32[]{:S(2)}, u32[]{:S(2)}) collective-permute-start(bf16[2,1,64,128]{3,2,1,0:T(8,128)(2,1)S(1)} %collective-permute-done.24.refs_6_), channel_id=1, source_target_pairs={{0,1},{1,0},{2,3},{3,2},{4,5},{5,4},{6,7},{7,6},{8,9},{9,8},{10,11... | collective-permute-start | bytes 98312 | tf_op jit(solution)/shard_map/ppermute | solution.py:413
  109.0 2.7 %collective-permute-start.29 = (bf16[2,1,64,128]{3,2,1,0:T(8,128)(2,1)S(1)}, bf16[2,1,64,128]{3,2,1,0:T(8,128)(2,1)S(1)}, u32[]{:S(2)}, u32[]{:S(2)}) collective-permute-start(bf16[2,1,64,128]{3,2,1,0:T(8,128)(2,1)S(1)} %collective-permute-done.25.refs_7_), channel_id=1, source_target_pairs={{0,1},{1,0},{2,3},{3,2},{4,5},{5,4},{6,7},{7,6},{8,9},{9,8},{10,11... | collective-permute-start | bytes 98312 | tf_op jit(solution)/shard_map/ppermute | solution.py:413
  (6 other events, 47.9 us)
where the time goes:
time: 114 us
  starting transfers between devices  59.1 us (52%)
  waiting for transfers between devices  25.5 us (22%)
  Pallas kernels  25.3 us (22%)
  local copies, waits for them, and re-layouts  3.36 us (3%)
    ppermute x9, starting transfers between devices, along(): return lax.ppermute(value, 'seq', route)  42.5 us
    pallas_call x12, Pallas kernels, call(): pl.pallas_call(kernel, out_shape=[jax.ShapeDtypeStruct(shape, dtype) for...  25.3 us
    ppermute x21, waiting for transfers between devices, to_peer(): return lax.ppermute(value, 'tp', [(i, i ^ flip) for i in range(tp)])  20.6 us
    ppermute x21, starting transfers between devices, to_peer(): return lax.ppermute(value, 'tp', [(i, i ^ flip) for i in range(tp)])  16.5 us
    ppermute x9, waiting for transfers between devices, along(): return lax.ppermute(value, 'seq', route)  4.86 us
    unnamed x18, local copies, waits for them, and re-layouts  3.36 us
  transfers between devices with their start and end apart: 30, of which 9 were waited for; matrix products, arithmetic and copies ran while one was open for 1% of the time, Pallas kernels for 20%

commit v1 on v0

--- a/solution.py
+++ b/solution.py
@@ -67,35 +67,40 @@
     return pl.ds(pl.multiple_of(base + index * ROWS, ROWS), ROWS)
 
 
-def cut_kernel(weight_ref, out_ref):
+def cut_kernel(weight_ref, out_ref, sem):
     rows = out_ref.shape[0]
     place = lax.axis_index("seq") % 2 * rows
-    out_ref[...] = weight_ref[pl.ds(pl.multiple_of(place, rows), rows), :]
-
-
-def lookup_kernel(codes_ref, table_ref, mine_ref, other_ref):
-    count, half = mine_ref.shape[:2]
+    copy = pltpu.make_async_copy(weight_ref.at[pl.ds(pl.multiple_of(place, rows), rows), :], out_ref, sem)
+    copy.start()
+    copy.wait()
+
+
+def enter_kernel(
+    hidden_ref, weight_ref, codes_ref, table_hbm, mine_ref, other_ref, look_mine, look_other, table_ref, sems,
+):
+    count, half = look_mine.shape[:2]
     vocab = table_ref.shape[1]
     core = lax.axis_index("tp") % 2
-    low = codes_ref[pl.ds(pl.multiple_of(core * half, half), half), :]
-    high = codes_ref[pl.ds(pl.multiple_of((1 - core) * half, half), half), :]
-    codes = jnp.concatenate([low, high], axis=0)
+    copies = [pltpu.make_async_copy(table_hbm.at[k], table_ref.at[k], sems.at[k]) for k in range(count)]
+    for copy in copies:
+        copy.start()
+    low = pl.ds(pl.multiple_of(core * half, half), half)
+    high = pl.ds(pl.multiple_of((1 - core) * half, half), half)
+    partial = dot(jnp.concatenate([hidden_ref[low, :], hidden_ref[high, :]], axis=0), weight_ref[...])
+    mine_ref[...] = partial[:half]
+    other_ref[...] = partial[half:].astype(BF16)
+    codes = jnp.concatenate([codes_ref[low, :], codes_ref[high, :]], axis=0)
     lanes = lax.broadcasted_iota(jnp.int32, (2 * half, vocab), 1)
     for k in range(count):
         chosen = jnp.where(lanes == codes[:, k : k + 1], 1.0, 0.0).astype(BF16)
+        copies[k].wait()
         found = dot(chosen, table_ref[k]).astype(BF16)
-        mine_ref[k] = found[:half]
-        other_ref[k] = found[half:]
-
-
-def context_kernel(hidden_ref, weight_ref, mine_ref, other_ref):
-    half = mine_ref.shape[0]
-    core = lax.axis_index("tp") % 2
-    low = hidden_ref[pl.ds(pl.multiple_of(core * half, half), half), :]
-    high = hidden_ref[pl.ds(pl.multiple_of((1 - core) * half, half), half), :]
-    partial = dot(jnp.concatenate([low, high], axis=0), weight_ref[...])
-    mine_ref[...] = partial[:half]
-    other_ref[...] = partial[half:].astype(BF16)
+        look_mine[k] = found[:half]
+        look_other[k] = found[half:]
+
+
+def join_kernel(mine_ref, other_ref, out_ref):
+    out_ref[...] = (mine_ref[...] + other_ref[...].astype(F32)).astype(BF16)
 
 
 def attention_kernel(
@@ -162,15 +167,10 @@
         lax.fori_loop(0, chunks, weigh, 0)
 
 
-def head_kernel(
-    att_mine, att_theirs, own_ref, pair_ref, part_a, part_b, part_c, part_d, stream_ref, gain_ref, codes_ref, head_mine, head_pair,
-    mid_ref, expo_ref, stats_ref, full_ref, mixed_ref, normed_ref, logit_ref,
+def mix_kernel(
+    att_ref, own_ref, pair_ref, part_a, part_b, part_c, part_d, stream_ref, full_ref, mixed_ref, sum_ref,
 ):
     steps, half, _ = stream_ref.shape
-    rank = lax.axis_index("tp")
-    core = rank % 2
-    vocab = head_mine.shape[2]
-    chunks = half // ROWS
     lanes, cut = own_ref.shape[0], part_a.shape[0]
     place = lax.axis_index("seq") % 2
     full_ref[0:lanes, :] = own_ref[...]
@@ -178,9 +178,22 @@
     for base, first, second in ((2 * lanes, part_a, part_b), (3 * lanes, part_c, part_d)):
         full_ref[pl.ds(pl.multiple_of(base + place * cut, cut), cut), :] = first[...]
         full_ref[pl.ds(pl.multiple_of(base + (1 - place) * cut, cut), cut), :] = second[...]
-    mixed_ref[...] = dot(att_mine[...], full_ref[0 : 2 * lanes, :]) + dot(
-        att_theirs[...], full_ref[2 * lanes : 4 * lanes, :]
-    )
+    sum_ref[...] = dot(att_ref[...], full_ref[0 : 2 * lanes, :])
+    for k in range(steps):
+        mixed_ref[k] = stream_ref[k] + sum_ref[k * half : (k + 1) * half, :]
+
+
+def head_kernel(
+    att_theirs, full_ref, stream_ref, gain_ref, codes_ref, head_mine, head_pair,
+    mid_ref, expo_ref, stats_ref, mixed_ref, normed_ref, logit_ref,
+):
+    steps, half, _ = stream_ref.shape
+    rank = lax.axis_index("tp")
+    core = rank % 2
+    vocab = head_mine.shape[2]
+    chunks = half // ROWS
+    middle = full_ref.shape[0] // 2
+    mixed_ref[...] = dot(att_theirs[...], full_ref[middle : 2 * middle, :])
 
     def enter(i, carry):
         for k in range(steps):
@@ -229,7 +242,7 @@
 
 def mid_kernel(
     frames_total, both_ref, mid_ref, gain_ref, stats_ref, stats_side, out_ref,
-    send_ref, keep_ref, sum_ref, loss_ref, low_ref,
+    send_ref, low_ref, sum_ref, loss_ref,
 ):
     steps, half, _ = mid_ref.shape
 
@@ -259,13 +272,24 @@
     lax.fori_loop(0, half // ROWS, leave, 0)
     middle = out_ref.shape[0] // 2
     send_ref[...] = dot_t(low_ref[...], out_ref[middle : 2 * middle, :]).astype(BF16)
-    keep_ref[...] = dot_t(low_ref[...], out_ref[0:middle, :])
+
+
+def keep_kernel(low_ref, out_ref, loss_mine, loss_pair, keep_ref, loss_ref):
+    half = loss_mine.shape[0]
+    core = lax.axis_index("tp") % 2
+    loss_ref[pl.ds(pl.multiple_of(core * half, half), half), :] = loss_mine[...]
+    loss_ref[pl.ds(pl.multiple_of((1 - core) * half, half), half), :] = loss_pair[...]
+    keep_ref[...] = dot_t(low_ref[...], out_ref[0 : out_ref.shape[0] // 2, :])
 
 
 def attention_back_kernel(
     head_dim, keep_ref, recv_ref, proj_mine, proj_pair, soft_mine, soft_pair, qkv_mine, qkv_pair,
-    stream_ref, gain_ref, sum_ref, part_ref, grad_ref, product_ref, prob_ref, back_mine, back_pair, normin_ref,
+    stream_ref, gain_ref, sum_ref, part_ref, *refs,
 ):
+    blocks_ref, grad_ref, product_ref, prob_ref, back_mine, back_pair, normin_ref = refs[-7:]
+    sends = refs[:-7]
+    radix = len(sends) + 1
+    digit = lax.axis_index("seq") % radix
     steps, half, _ = stream_ref.shape
     lanes = keep_ref.shape[1] // 2
     chunks = half // ROWS
@@ -325,23 +349,40 @@
         part = sum_ref[chunk(i), :]
         for k in range(steps):
             part = part + norm_back(stream_ref[k, chunk(i), :], gain_ref[...], normin_ref[at_row(k * half, i), :])
-        part_ref[chunk(i), :] = part.astype(BF16)
+        part = part.astype(BF16)
+        part_ref[chunk(i), :] = part
+        count, _, size = blocks_ref.shape
+        for j in range(count):
+            blocks_ref[j, chunk(i), :] = part[:, j * size : (j + 1) * size]
         return carry
 
     lax.fori_loop(0, chunks, leave, 0)
-
-
-def sum_kernel(radix, low, part_ref, side_ref, grad_ref, *refs):
-    outs, blocks_ref = refs[:radix], refs[radix]
+    for shift, out in enumerate(sends):
+        for w in range(out.shape[0]):
+            out[w] = blocks_ref[w * radix + (digit + shift + 1) % radix]
+
+
+def sum_kernel(first, radix, *refs):
+    part_ref, side_ref = refs[:2]
+    near, far = refs[2 : first + 1], refs[first + 1 : 2 * first]
+    grad_ref, *outs = refs[2 * first : 2 * first + 1 + radix]
+    blocks_ref, held_ref = refs[2 * first + 1 + radix :]
     count, _, size = blocks_ref.shape
-    digit = lax.axis_index("seq") // low % radix
+    rest = count // first
+    digit = lax.axis_index("seq") % first
+    upper = lax.axis_index("seq") // first % radix
     grad = (part_ref[...].astype(F32) + side_ref[...].astype(F32)).astype(BF16)
     grad_ref[...] = grad
     for j in range(count):
         blocks_ref[j] = grad[:, j * size : (j + 1) * size]
+    for w in range(rest):
+        held_ref[0, w] = blocks_ref[w * first + digit]
+    for place, (one, two) in enumerate(zip(near, far)):
+        held_ref[place + 1] = (one[...].astype(F32) + two[...].astype(F32)).astype(BF16)
     for shift, out in enumerate(outs):
-        for w in range(count // radix):
-            out[0, w] = blocks_ref[w * radix + (digit + shift) % radix]
+        for i in range(first):
+            for w in range(rest // radix):
+                out[i, w] = held_ref[i, w * radix + (upper + shift) % radix]
 
 
 def pick_kernel(count, radix, low, *refs):
@@ -355,33 +396,40 @@
                 place += 1
 
 
-def hidden_grad_kernel(mine_ref, pair_ref, loss_mine, loss_pair, weight_ref, out_ref, loss_ref, full_ref):
+def hidden_grad_kernel(mine_ref, pair_ref, weight_ref, out_ref, full_ref):
     half = mine_ref.shape[0]
     core = lax.axis_index("tp") % 2
-    low = pl.ds(pl.multiple_of(core * half, half), half)
-    high = pl.ds(pl.multiple_of((1 - core) * half, half), half)
-    full_ref[low, :] = mine_ref[...]
-    full_ref[high, :] = pair_ref[...]
-    loss_ref[low, :] = loss_mine[...]
-    loss_ref[high, :] = loss_pair[...]
+    full_ref[pl.ds(pl.multiple_of(core * half, half), half), :] = mine_ref[...]
+    full_ref[pl.ds(pl.multiple_of((1 - core) * half, half), half), :] = pair_ref[...]
     out_ref[...] = dot_t(full_ref[...], weight_ref[...]).astype(BF16)
 
 
-def project_kernel(count, *refs):
-    states, mine, pair = refs[:count], refs[count : 2 * count], refs[2 * count : 3 * count]
-    out_ref, grads_ref = refs[3 * count :]
+def project_kernel(radices, *refs):
+    count = radices[-1]
+    out_ref, grads_ref = refs[-2:]
+    mine, pair = refs[-2 - 2 * count : -2 - count], refs[-2 - count : -2]
+    states = refs[: -2 - 2 * count]
     half = mine[0].shape[2]
     core = lax.axis_index("tp") % 2
+    index = lax.axis_index("seq")
+    held = mine[0].shape[0]
     for p, (low, high) in enumerate(zip(mine, pair)):
-        for q in range(low.shape[0]):
-            base = 2 * q * half
-            grads_ref[p, pl.ds(pl.multiple_of(base + core * half, half), half), :] = low[q, 0]
-            grads_ref[p, pl.ds(pl.multiple_of(base + (1 - core) * half, half), half), :] = high[q, 0]
+        for q in range(held):
+            grads_ref[p * held + q, pl.ds(pl.multiple_of(core * half, half), half), :] = low[q, 0]
+            grads_ref[p * held + q, pl.ds(pl.multiple_of((1 - core) * half, half), half), :] = high[q, 0]
     total = 0.0
-    for p, rows in enumerate(states):
+    for p in range(count * held):
+        if len(states) > 1:
+            rows = states[p][0]
+        else:
+            source, left, low = 0, p, 1
+            for radix in radices:
+                source = source + (index // low + radix - left % radix) % radix * low
+                left //= radix
+                low *= radix
+            rows = states[0][source]
         total = total + lax.dot_general(
-            grads_ref[p], rows[...].reshape(-1, rows.shape[2]),
-            (((0,), (0,)), ((), ())), preferred_element_type=F32,
+            grads_ref[p], rows, (((0,), (0,)), ((), ())), preferred_element_type=F32
         )
     out_ref[...] = total.T
 
@@ -412,27 +460,29 @@
     def to_peer(value, flip):
         return lax.ppermute(value, "tp", [(i, i ^ flip) for i in range(tp)])
 
-    def along(value, low, radix, shift):
+    def along(value, low, radix, shift, flip=0):
         route = []
         for i in range(seq):
             digit = i // low % radix
-            route.append((i, i + ((digit + shift) % radix - digit) * low))
-        return lax.ppermute(value, "seq", route)
+            there = i + ((digit + shift) % radix - digit) * low
+            route += [(i * tp + j, there * tp + (j ^ flip)) for j in range(tp)]
+        return lax.ppermute(value, ("seq", "tp"), route)
 
     cut = lanes // 2
-    (out_part,) = call(cut_kernel, [((cut, width), BF16)], [], (w_out,), 6 * 10**9, limit=4)
+    (out_part,) = call(
+        cut_kernel, [((cut, width), BF16)], [pltpu.SemaphoreType.DMA], (w_out,), 6 * 10**9, {0: pltpu.HBM}, limit=4
+    )
     out_part = to_peer(out_part, 2)
-    partial, partial_other = call(
-        context_kernel, [((half, width), F32), ((half, width), BF16)], [],
-        (hidden, w_proj), 6 * 10**9,
-    )
-    looked, looked_other = call(
-        lookup_kernel,
-        [((steps - 1, half, lanes), BF16)] * 2,
-        [],
-        (codes, embed_table), 2 * frames * embed_table.size,
-    )
-    partial = (partial + to_peer(partial_other, 1).astype(F32)).astype(BF16)
+    partial, partial_other, looked, looked_other = call(
+        enter_kernel,
+        [((half, width), F32), ((half, width), BF16)] + [((steps - 1, half, lanes), BF16)] * 2,
+        [pltpu.VMEM(embed_table.shape, BF16), pltpu.SemaphoreType.DMA((steps - 1,))],
+        (hidden, w_proj, codes, embed_table), 6 * 10**9, {3: pltpu.HBM}, limit=60,
+    )
+    (partial,) = call(
+        join_kernel, [((half, width), BF16)], [],
+        (partial, to_peer(partial_other, 1)), partial.size, limit=4,
+    )
     partial_side = to_peer(partial, 2)
     looked = [looked, to_peer(looked_other, 1), to_peer(looked, 2), to_peer(looked_other, 3)]
 
@@ -444,12 +494,18 @@
         w_out, to_peer(w_out, 1), out_part, out_rest,
         to_peer(out_part, 1), to_peer(out_rest, 1),
     )
-    states = [hidden[None]]
-    low = 1
-    for radix in seq_radices(seq):
-        gathered = jnp.concatenate(states, axis=0)
-        states = [gathered] + [along(gathered, low, radix, shift) for shift in range(1, radix)]
-        low *= radix
+    radices = seq_radices(seq)
+    if seq > 16:
+        states = [lax.all_gather(hidden, "seq")]
+    else:
+        states, low = [hidden[None]], seq
+        for radix in reversed(radices):
+            low //= radix
+            states = [
+                item if shift == 0 else along(item, low, radix, shift)
+                for item in states
+                for shift in range(radix)
+            ]
 
     stream_in, att_mine, proj_mine, proj_pair, soft_mine, soft_pair = call(
         functools.partial(attention_kernel, head_dim),
@@ -464,35 +520,44 @@
         (partial, partial_side, *looked, qkv_mine, qkv_pair, gain_attn), 4 * rows * qkv_mine.size,
     )
     att_theirs = to_peer(att_mine, 2)
-    stream_mid, expo, stats, out_full = call(
+    out_full, mixed = call(
+        mix_kernel, [((tp * lanes, width), BF16), ((steps, half, width), F32)],
+        [pltpu.VMEM((rows, width), F32)],
+        (att_mine, *out_parts, stream_in), rows * width * width,
+    )
+    stream_mid, expo, stats = call(
         head_kernel,
-        [((steps, half, width), F32), ((steps, 2 * half, 2 * vocab_local), BF16), ((half, 128), F32),
-         ((tp * lanes, width), BF16)],
+        [((steps, half, width), F32), ((steps, 2 * half, 2 * vocab_local), BF16), ((half, 128), F32)],
         [
             pltpu.VMEM((rows, width), F32),
             pltpu.VMEM((rows, width), BF16),
             pltpu.VMEM((steps, half, 2 * vocab_local), F32),
         ],
-        (att_mine, att_theirs, *out_parts, stream_in, gain_head, codes, head_table, head_pair),
-        4 * half * head_table.size + 2 * rows * width * width,
+        (att_theirs, out_full, mixed, gain_head, codes, head_table, head_pair),
+        4 * half * head_table.size + rows * width * width,
     )
     stats_side = to_peer(stats, 2)
     (both,) = call(
         head_back_kernel, [((steps, 2 * half, width), F32)], [],
         (expo, head_table, head_pair), 8 * half * head_table.size,
     )
-    att_send, att_keep, mid_sum, losses = call(
+    att_send, mid_low, mid_sum, losses = call(
         functools.partial(mid_kernel, total),
-        [((rows, 2 * lanes), BF16), ((rows, 2 * lanes), F32), ((half, width), F32), ((half, steps), F32)],
-        [pltpu.VMEM((rows, width), BF16)],
-        (both, stream_mid, gain_head, stats, stats_side, out_full),
-        2 * rows * width * width,
+        [((rows, 2 * lanes), BF16), ((rows, width), BF16), ((half, width), F32), ((half, steps), F32)],
+        [], (both, stream_mid, gain_head, stats, stats_side, out_full), rows * width * width,
     )
     att_recv = to_peer(att_send, 2)
-    (part,) = call(
+    att_keep, row_loss = call(
+        keep_kernel, [((rows, 2 * lanes), F32), ((frames, steps), F32)], [],
+        (mid_low, out_full, losses, to_peer(losses, 1)), rows * width * width,
+    )
+    size = width // seq
+    first, rest = radices[0], seq // radices[0]
+    part, *sends = call(
         functools.partial(attention_back_kernel, head_dim),
-        [((half, width), BF16)],
+        [((half, width), BF16)] + [((rest, half, size), BF16)] * (first - 1),
         [
+            pltpu.VMEM((seq, half, size), BF16),
             pltpu.VMEM((rows, lanes), BF16),
             pltpu.VMEM((pairs * half, lanes), BF16),
             pltpu.VMEM((pairs * half, lanes), F32),
@@ -504,19 +569,22 @@
          stream_in, gain_attn, mid_sum),
         4 * rows * qkv_mine.size,
     )
-    size = width // seq
-    radices = seq_radices(seq)
-    low, rest = 1, seq // radices[0]
     part_side = to_peer(part, 2)
+    near = [along(item, 1, first, shift + 1) for shift, item in enumerate(sends)]
+    far = [along(item, 1, first, shift + 1, 2) for shift, item in enumerate(sends)]
+    part_side, *states = lax.optimization_barrier((part_side, *states))
     context_grad, *sends = call(
-        functools.partial(sum_kernel, radices[0], 1),
-        [((half, width), BF16)] + [((1, rest, half, size), BF16)] * radices[0],
-        [pltpu.VMEM((seq, half, size), BF16)],
-        (part, part_side), part.size, limit=4,
-    )
+        functools.partial(sum_kernel, first, radices[1]),
+        [((half, width), BF16)] + [((first, rest // radices[1], half, size), BF16)] * radices[1],
+        [pltpu.VMEM((seq, half, size), BF16), pltpu.VMEM((first, rest, half, size), BF16)],
+        (part, part_side, *near, *far), part.size, limit=4,
+    )
+    low = first
     for stage, radix in enumerate(radices):
-        if stage > 0:
-            rest //= radix
+        if stage == 0:
+            continue
+        rest //= radix
+        if stage > 1:
             held = sum(item.shape[0] for item in owned)
             sends = call(
                 functools.partial(pick_kernel, len(owned), radix, low),
@@ -524,19 +592,16 @@
             )
         owned = [sends[0]] + [along(item, low, radix, shift + 1) for shift, item in enumerate(sends[1:])]
         low *= radix
-    grad_hidden, row_loss = call(
-        hidden_grad_kernel,
-        [((frames, w_proj.shape[0]), BF16), ((frames, steps), F32)],
+    (grad_hidden,) = call(
+        hidden_grad_kernel, [((frames, w_proj.shape[0]), BF16)],
         [pltpu.VMEM((frames, width), BF16)],
-        (context_grad, to_peer(context_grad, 1), losses, to_peer(losses, 1), w_proj),
-        2 * frames * w_proj.size,
+        (context_grad, to_peer(context_grad, 1), w_proj), 2 * frames * w_proj.size,
     )
     paired = [to_peer(item, 1) for item in owned]
-    held = states[0].shape[0]
     (grad_proj,) = call(
-        functools.partial(project_kernel, len(states)),
+        functools.partial(project_kernel, tuple(radices)),
         [((hidden.shape[1], size), F32)],
-        [pltpu.VMEM((len(states), held * frames, size), BF16)],
+        [pltpu.VMEM((seq, frames, size), BF16)],
         (*states, *owned, *paired), 2 * frames * seq * hidden.shape[1] * size, limit=40 if seq > 16 else 12,
     )
     return (row_loss, grad_hidden, grad_proj)

time: 114 us -> 100 us (0.88)
  starting transfers between devices: 59.1 us -> 33.2 us
  local copies, waits for them, and re-layouts: 3.36 us -> 10.5 us
  Pallas kernels: 25.3 us -> 29.7 us
    ppermute x9 -> x13, starting transfers between devices: 42.5 us -> 20.9 us  [along(): return lax.ppermute(value, ('seq', 'tp'), route)]
    ppermute x21, waiting for transfers between devices: 20.6 us -> 11.9 us  [to_peer(): return lax.ppermute(value, 'tp', [(i, i ^ flip) for i in range(tp)])]
    ppermute x9 -> x13, waiting for transfers between devices: 4.86 us -> 13.4 us  [along(): return lax.ppermute(value, ('seq', 'tp'), route)]
    unnamed x18 -> x46, local copies, waits for them, and re-layouts: 3.36 us -> 10.5 us
    pallas_call x12 -> x13, Pallas kernels: 25.3 us -> 29.7 us  [call(): pl.pallas_call(kernel, out_shape=[jax.ShapeDtypeStruct(shape, dtype) for...]
    ppermute x21, starting transfers between devices: 16.5 us -> 12.3 us  [to_peer(): return lax.ppermute(value, 'tp', [(i, i ^ flip) for i in range(tp)])]
  transfers between devices with their start and end apart: 30 -> 34, of which waited for: 9 -> 12; matrix products, arithmetic and copies ran while one was open for 1% -> 1% of each run, Pallas kernels for 20% -> 28%
where the time goes in v1:
time: 100 us; the launch traced here: 99.6 us
  starting transfers between devices  33.2 us (33%)
  Pallas kernels  29.7 us (30%)
  waiting for transfers between devices  25.3 us (25%)
  local copies, waits for them, and re-layouts  10.5 us (10%)
    pallas_call x13, Pallas kernels, call(): pl.pallas_call(kernel, out_shape=[jax.ShapeDtypeStruct(shape, dtype) for...  29.7 us
    ppermute x13, starting transfers between devices, along(): return lax.ppermute(value, ('seq', 'tp'), route)  20.9 us
    ppermute x13, waiting for transfers between devices, along(): return lax.ppermute(value, ('seq', 'tp'), route)  13.4 us
    ppermute x21, starting transfers between devices, to_peer(): return lax.ppermute(value, 'tp', [(i, i ^ flip) for i in range(tp)])  12.3 us
    ppermute x21, waiting for transfers between devices, to_peer(): return lax.ppermute(value, 'tp', [(i, i ^ flip) for i in range(tp)])  11.9 us
    unnamed x46, local copies, waits for them, and re-layouts  10.5 us
  transfers between devices with their start and end apart: 34, of which 12 were waited for; matrix products, arithmetic and copies ran while one was open for 1% of the time, Pallas kernels for 28%

profile of v1, /device:TPU:0, one launch (start us, length us, event | category | flops | bytes accessed | tf_op | source)
XLA Modules:
  0.0 99.6 jit_solution(12198541838226149510)
XLA Ops:
  2.4 3.0 %collective-permute-start.8 = (bf16[128,1024]{1,0:T(8,128)(2,1)S(1)}, bf16[128,1024]{1,0:T(8,128)(2,1)}, u32[]{:S(2)}, u32[]{:S(2)}) collective-permute-start(bf16[128,1024]{1,0:T(8,128)(2,1)S(1)} %shard_map.115), channel_id=1, source_target_pairs={{0,2},{1,3},{2,0},{3,1},{4,6},{5,7},{6,4},{7,5},{8,10},{9,11},{10,... | collective-permute-start | bytes 786440 | tf_op jit(solution)/shard_map/ppermute | solution.py:461
  6.1 4.9 %shard_map.112 = (f32[64,1024]{1,0:T(8,128)}, bf16[64,1024]{1,0:T(8,128)(2,1)}, bf16[3,64,256]{2,1,0:T(8,128)(2,1)}, bf16[3,64,256]{2,1,0:T(8,128)(2,1)}) custom-call(bf16[128,1024]{1,0:T(8,128)(2,1)} %hidden_ref.1, bf16[1024,1024]{1,0:T(8,128)(2,1)} %weight_ref.5, s32[128,4]{1,0:T(8,128)} %copy.12.codes_ref, bf16[3,2048,256]{2,1,0:T(8,128)(2,1)} %table_hbm.1), custom_call_target="tpu_custom_call" | custom-call | flops 6000000000 | bytes 20000000 | tf_op jit(solution)/shard_map/pallas_call | solution.py:51
  13.4 1.5 %collective-permute-start.9 = (bf16[128,1024]{1,0:T(8,128)(2,1)}, bf16[128,1024]{1,0:T(8,128)(2,1)S(1)}, u32[]{:S(2)}, u32[]{:S(2)}) collective-permute-start(bf16[128,1024]{1,0:T(8,128)(2,1)} %collective-permute-done.8.part_a), channel_id=1, source_target_pairs={{0,4},{1,5},{2,6},{3,7},{4,0},{5,1},{6,2},{7,3},{8,12},{9,13},{10,... | collective-permute-start | bytes 786440 | tf_op jit(solution)/shard_map/ppermute | solution.py:469
  14.9 2.7 %collective-permute-done.3.look2 = bf16[3,64,256]{2,1,0:T(8,128)(2,1)S(1)} collective-permute-done((bf16[3,64,256]{2,1,0:T(8,128)(2,1)}, bf16[3,64,256]{2,1,0:T(8,128)(2,1)S(1)}, u32[]{:S(2)}, u32[]{:S(2)}) %collective-permute-start.3) | collective-permute-done | bytes 98336 | tf_op jit(solution)/shard_map/ppermute | solution.py:461
  19.6 2.8 %collective-permute-done.4.look3 = bf16[3,64,256]{2,1,0:T(8,128)(2,1)S(1)} collective-permute-done((bf16[3,64,256]{2,1,0:T(8,128)(2,1)}, bf16[3,64,256]{2,1,0:T(8,128)(2,1)S(1)}, u32[]{:S(2)}, u32[]{:S(2)}) %collective-permute-start.4) | collective-permute-done | bytes 98336 | tf_op jit(solution)/shard_map/ppermute | solution.py:461
  22.4 1.1 %collective-permute-start.1 = (bf16[64,1024]{1,0:T(8,128)(2,1)S(1)}, bf16[64,1024]{1,0:T(8,128)(2,1)S(1)}, u32[]{:S(2)}, u32[]{:S(2)}) collective-permute-start(bf16[64,1024]{1,0:T(8,128)(2,1)S(1)} %shard_map.113.own_ref), channel_id=1, source_target_pairs={{0,2},{1,3},{2,0},{3,1},{4,6},{5,7},{6,4},{7,5},{8,10},{9,11},{10,... | collective-permute-start | bytes 393224 | tf_op jit(solution)/shard_map/ppermute | solution.py:461
  23.5 3.9 %collective-permute-done.1.side_ref = bf16[64,1024]{1,0:T(8,128)(2,1)S(1)} collective-permute-done((bf16[64,1024]{1,0:T(8,128)(2,1)S(1)}, bf16[64,1024]{1,0:T(8,128)(2,1)S(1)}, u32[]{:S(2)}, u32[]{:S(2)}) %collective-permute-start.1) | collective-permute-done | bytes 131104 | tf_op jit(solution)/shard_map/ppermute | solution.py:461
  28.8 3.3 %shard_map.114 = (f32[4,64,1024]{2,1,0:T(8,128)S(1)}, bf16[256,512]{1,0:T(8,128)(2,1)S(1)}, bf16[256,768]{1,0:T(8,128)(2,1)S(1)}, bf16[256,768]{1,0:T(8,128)(2,1...) custom-call(bf16[64,1024]{1,0:T(8,128)(2,1)S(1)} %shard_map.113.own_ref, ...), custom_call_target="tpu_custom_call" | custom-call | flops 805306368 | bytes 2684354 | tf_op jit(solution)/shard_map/pallas_call | solution.py:51
  32.1 1.4 %collective-permute-start.6 = (bf16[256,512]{1,0:T(8,128)(2,1)S(1)}, bf16[256,512]{1,0:T(8,128)(2,1)S(1)}, u32[]{:S(2)}, u32[]{:S(2)}) collective-permute-start(bf16[256,512]{1,0:T(8,128)(2,1)S(1)} %get-tuple-element.44.att_ref), channel_id=1, source_target_pairs={{0,2},{1,3},{2,0},{3,1},{4,6},{5,7},{6,4},{7,5},{8,10},{9,11},{10,... | collective-permute-start | bytes 786440 | tf_op jit(solution)/shard_map/ppermute | solution.py:461
  33.5 1.6 %collective-permute-start.18 = (bf16[1,128,1024]{2,1,0:T(8,128)(2,1)S(1)}, bf16[1,128,1024]{2,1,0:T(8,128)(2,1)S(1)}, u32[]{:S(2)}, u32[]{:S(2)}) collective-permute-start(bf16[1,128,1024]{2,1,0:T(8,128)(2,1)S(1)} %bitcast.7), channel_id=1, source_target_pairs={{0,8},{1,9},{2,10},{3,11},{4,12},{5,13},{6,14},{7,15},{8,16},{9,17... | collective-permute-start | bytes 786440 | tf_op jit(solution)/shard_map/ppermute | solution.py:469
  35.1 2.6 %collective-permute-start.20 = (bf16[1,128,1024]{2,1,0:T(8,128)(2,1)S(1)}, bf16[1,128,1024]{2,1,0:T(8,128)(2,1)S(1)}, u32[]{:S(2)}, u32[]{:S(2)}) collective-permute-start(bf16[1,128,1024]{2,1,0:T(8,128)(2,1)S(1)} %bitcast.8), channel_id=1, source_target_pairs={{0,16},{1,17},{2,18},{3,19},{4,20},{5,21},{6,22},{7,23},{8,24},{9,... | collective-permute-start | bytes 786440 | tf_op jit(solution)/shard_map/ppermute | solution.py:469
  37.7 1.4 %collective-permute-start.22 = (bf16[1,128,1024]{2,1,0:T(8,128)(2,1)S(1)}, bf16[1,128,1024]{2,1,0:T(8,128)(2,1)S(1)}, u32[]{:S(2)}, u32[]{:S(2)}) collective-permute-start(bf16[1,128,1024]{2,1,0:T(8,128)(2,1)S(1)} %bitcast.9), channel_id=1, source_target_pairs={{0,24},{1,25},{2,26},{3,27},{4,28},{5,29},{6,30},{7,31},{8,0},{9,1... | collective-permute-start | bytes 786440 | tf_op jit(solution)/shard_map/ppermute | solution.py:469
  39.1 1.5 %shard_map.116 = (bf16[1024,1024]{1,0:T(8,128)(2,1)S(1)}, f32[4,64,1024]{2,1,0:T(8,128)S(1)}) custom-call(bf16[256,512]{1,0:T(8,128)(2,1)S(1)} %get-tuple-element.44.att_ref, bf16[256,1024]{1,0:T(8,128)(2,1)S(1)} %copy-done.4, bf16[256,1024]{1,0:T(8,128)(2,1)S(1)} %collective-permute-done.7.pair_ref, bf16[128,1024]{1,0:T(8,128)(2,1)} %collective-permute-done.8.part_a, ...), custom_call_target="tpu_custom_call" | custom-call | flops 268435456 | bytes 894784 | tf_op jit(solution)/shard_map/pallas_call | solution.py:51
  40.6 5.7 %shard_map.117 = (f32[4,64,1024]{2,1,0:T(8,128)S(1)}, bf16[4,128,1024]{2,1,0:T(8,128)(2,1)S(1)}, f32[64,128]{1,0:T(8,128)S(1)}) custom-call(bf16[256,512]{1,0:T(8,128)(2,1)S(1)} %collective-permute-done.6.att_theirs, bf16[1024,1024]{1,0:T(8,128)(2,1)S(1)} %get-tuple-element.46.full_ref.out_ref, f32[4,64,1024]{2,1,0:T(8,128)S(1)} %get-tuple-element.47.stream_ref, ...), custom_call_target="tpu_custom_call" | custom-call | flops 805306368 | bytes 2684354 | tf_op jit(solution)/shard_map/pallas_call | solution.py:51
  46.4 1.2 %collective-permute-start.13 = (f32[64,128]{1,0:T(8,128)S(1)}, f32[64,128]{1,0:T(8,128)S(1)}, u32[]{:S(2)}, u32[]{:S(2)}) collective-permute-start(f32[64,128]{1,0:T(8,128)S(1)} %get-tuple-element.50.stats_ref), channel_id=1, source_target_pairs={{0,2},{1,3},{2,0},{3,1},{4,6},{5,7},{6,4},{7,5},{8,10},{9,11},{10,... | collective-permute-start | bytes 98312 | tf_op jit(solution)/shard_map/ppermute | solution.py:461
  47.6 5.0 %shard_map.118.both_ref = f32[4,128,1024]{2,1,0:T(8,128)S(1)} custom-call(bf16[4,128,1024]{2,1,0:T(8,128)(2,1)S(1)} %get-tuple-element.48.expo_ref, bf16[4,1024,512]{2,1,0:T(8,128)(2,1)S(1)} %copy-done, bf16[4,1024,512]{2,1,0:T(8,128)(2,1)} %collective-permute-done.12.head_pair), custom_call_target="tpu_custom_call" | custom-call | flops 1073741824 | bytes 3579139 | tf_op jit(solution)/shard_map/pallas_call | solution.py:51
  52.6 2.3 %shard_map.119 = (bf16[256,512]{1,0:T(8,128)(2,1)S(1)}, bf16[256,1024]{1,0:T(8,128)(2,1)S(1)}, f32[64,1024]{1,0:T(8,128)S(1)}, f32[64,4]{1,0:T(8,128)S(1)}) custom-call(f32[4,128,1024]{2,1,0:T(8,128)S(1)} %shard_map.118.both_ref, f32[4,64,1024]{2,1,0:T(8,128)S(1)} %get-tuple-element.49.mid_ref, f32[1,1024]{1,0:T(1,128)S(1)} %bitcast.13, ...), custom_call_target="tpu_custom_call" | custom-call | flops 268435456 | bytes 894784 | tf_op jit(solution)/shard_map/pallas_call | solution.py:51
  55.9 1.5 %collective-permute-start.17 = (bf16[1,128,1024]{2,1,0:T(8,128)(2,1)S(1)}, bf16[1,128,1024]{2,1,0:T(8,128)(2,1)S(1)}, u32[]{:S(2)}, u32[]{:S(2)}) collective-permute-start(bf16[1,128,1024]{2,1,0:T(8,128)(2,1)S(1)} %bitcast.10), channel_id=1, source_target_pairs={{0,4},{1,5},{2,6},{3,7},{4,0},{5,1},{6,2},{7,3},{8,12},{9,13},{10,... | collective-permute-start | bytes 786440 | tf_op jit(solution)/shard_map/ppermute | solution.py:469
  57.9 1.6 %collective-permute-start.21 = (bf16[1,128,1024]{2,1,0:T(8,128)(2,1)S(1)}, bf16[1,128,1024]{2,1,0:T(8,128)(2,1)S(1)}, u32[]{:S(2)}, u32[]{:S(2)}) collective-permute-start(bf16[1,128,1024]{2,1,0:T(8,128)(2,1)S(1)} %collective-permute-done.20.refs_4_), channel_id=1, source_target_pairs={{0,4},{1,5},{2,6},{3,7},{4,0},{5,1},{6,2},{7,3},{8,12},{9,13},{10,... | collective-permute-start | bytes 786440 | tf_op jit(solution)/shard_map/ppermute | solution.py:469
  59.5 1.1 %collective-permute-start.23 = (bf16[1,128,1024]{2,1,0:T(8,128)(2,1)S(1)}, bf16[1,128,1024]{2,1,0:T(8,128)(2,1)S(1)}, u32[]{:S(2)}, u32[]{:S(2)}) collective-permute-start(bf16[1,128,1024]{2,1,0:T(8,128)(2,1)S(1)} %collective-permute-done.22.refs_6_), channel_id=1, source_target_pairs={{0,4},{1,5},{2,6},{3,7},{4,0},{5,1},{6,2},{7,3},{8,12},{9,13},{10,... | collective-permute-start | bytes 786440 | tf_op jit(solution)/shard_map/ppermute | solution.py:469
  62.1 3.1 %shard_map.121 = (bf16[64,1024]{1,0:T(8,128)(2,1)S(1)}, bf16[4,64,128]{2,1,0:T(8,128)(2,1)S(1)}) custom-call(f32[256,512]{1,0:T(8,128)S(1)} %get-tuple-element.54.keep_ref, bf16[256,512]{1,0:T(8,128)(2,1)S(1)} %collective-permute-done.15.recv_ref, bf16[256,768]{1,0:T(8,128)(2,1)S(1)} %get-tuple-element.56.proj_mine, ...), custom_call_target="tpu_custom_call" | custom-call | flops 805306368 | bytes 2684354 | tf_op jit(solution)/shard_map/pallas_call | solution.py:51
  66.0 1.5 %collective-permute-start.24 = (bf16[4,64,128]{2,1,0:T(8,128)(2,1)S(1)}, bf16[4,64,128]{2,1,0:T(8,128)(2,1)S(1)}, u32[]{:S(2)}, u32[]{:S(2)}) collective-permute-start(bf16[4,64,128]{2,1,0:T(8,128)(2,1)S(1)} %get-tuple-element.63), channel_id=1, source_target_pairs={{0,4},{1,5},{2,6},{3,7},{4,0},{5,1},{6,2},{7,3},{8,12},{9,13},{10,... | collective-permute-start | bytes 196616 | tf_op jit(solution)/shard_map/ppermute | solution.py:469
  67.5 3.8 %collective-permute-done.19.refs_3_ = bf16[1,128,1024]{2,1,0:T(8,128)(2,1)S(1)} collective-permute-done((bf16[1,128,1024]{2,1,0:T(8,128)(2,1)S(1)}, bf16[1,128,1024]{2,1,0:T(8,128)(2,1)S(1)}, u32[]{:S(2)}, u32[]{:S(2)}) %collective-permute-start.19) | collective-permute-done | bytes 262176 | tf_op jit(solution)/shard_map/ppermute | solution.py:469
  71.4 2.1 %collective-permute-start.25 = (bf16[4,64,128]{2,1,0:T(8,128)(2,1)S(1)}, bf16[4,64,128]{2,1,0:T(8,128)(2,1)S(1)}, u32[]{:S(2)}, u32[]{:S(2)}) collective-permute-start(bf16[4,64,128]{2,1,0:T(8,128)(2,1)S(1)} %get-tuple-element.63), channel_id=1, source_target_pairs={{0,6},{1,7},{2,4},{3,5},{4,2},{5,3},{6,0},{7,1},{8,14},{9,15},{10,... | collective-permute-start | bytes 196616 | tf_op jit(solution)/shard_map/ppermute | solution.py:469
  73.5 4.2 %collective-permute-done.21.refs_5_ = bf16[1,128,1024]{2,1,0:T(8,128)(2,1)S(1)} collective-permute-done((bf16[1,128,1024]{2,1,0:T(8,128)(2,1)S(1)}, bf16[1,128,1024]{2,1,0:T(8,128)(2,1)S(1)}, u32[]{:S(2)}, u32[]{:S(2)}) %collective-permute-start.21) | collective-permute-done | bytes 262176 | tf_op jit(solution)/shard_map/ppermute | solution.py:469
  78.4 3.0 %collective-permute-done.23.refs_7_ = bf16[1,128,1024]{2,1,0:T(8,128)(2,1)S(1)} collective-permute-done((bf16[1,128,1024]{2,1,0:T(8,128)(2,1)S(1)}, bf16[1,128,1024]{2,1,0:T(8,128)(2,1)S(1)}, u32[]{:S(2)}, u32[]{:S(2)}) %collective-permute-start.23) | collective-permute-done | bytes 262176 | tf_op jit(solution)/shard_map/ppermute | solution.py:469
  82.3 1.6 %collective-permute-start.27 = (bf16[2,1,64,128]{3,2,1,0:T(8,128)(2,1)S(1)}, bf16[2,1,64,128]{3,2,1,0:T(8,128)(2,1)S(1)}, u32[]{:S(2)}, u32[]{:S(2)}) collective-permute-start(bf16[2,1,64,128]{3,2,1,0:T(8,128)(2,1)S(1)} %get-tuple-element.74), channel_id=1, source_target_pairs={{0,8},{1,9},{2,10},{3,11},{4,12},{5,13},{6,14},{7,15},{8,16},{9,17... | collective-permute-start | bytes 98312 | tf_op jit(solution)/shard_map/ppermute | solution.py:469
  83.9 2.6 %collective-permute-start.28 = (bf16[2,1,64,128]{3,2,1,0:T(8,128)(2,1)S(1)}, bf16[2,1,64,128]{3,2,1,0:T(8,128)(2,1)S(1)}, u32[]{:S(2)}, u32[]{:S(2)}) collective-permute-start(bf16[2,1,64,128]{3,2,1,0:T(8,128)(2,1)S(1)} %get-tuple-element.75), channel_id=1, source_target_pairs={{0,16},{1,17},{2,18},{3,19},{4,20},{5,21},{6,22},{7,23},{8,24},{9,... | collective-permute-start | bytes 98312 | tf_op jit(solution)/shard_map/ppermute | solution.py:469
  86.5 1.3 %collective-permute-start.29 = (bf16[2,1,64,128]{3,2,1,0:T(8,128)(2,1)S(1)}, bf16[2,1,64,128]{3,2,1,0:T(8,128)(2,1)S(1)}, u32[]{:S(2)}, u32[]{:S(2)}) collective-permute-start(bf16[2,1,64,128]{3,2,1,0:T(8,128)(2,1)S(1)} %get-tuple-element.76), channel_id=1, source_target_pairs={{0,24},{1,25},{2,26},{3,27},{4,28},{5,29},{6,30},{7,31},{8,0},{9,1... | collective-permute-start | bytes 98312 | tf_op jit(solution)/shard_map/ppermute | solution.py:469
  89.2 1.3 %collective-permute-done.29.refs_11_ = bf16[2,1,64,128]{3,2,1,0:T(8,128)(2,1)S(1)} collective-permute-done((bf16[2,1,64,128]{3,2,1,0:T(8,128)(2,1)S(1)}, bf16[2,1,64,128]{3,2,1,0:T(8,128)(2,1)S(1)}, u32[]{:S(2)}, u32[]{:S(2)}) %collective-permute-start.29) | collective-permute-done | bytes 32800 | tf_op jit(solution)/shard_map/ppermute | solution.py:469
  96.4 1.7 %shard_map.124 = f32[1024,128]{1,0:T(8,128)} custom-call(bf16[1,128,1024]{2,1,0:T(8,128)(2,1)S(1)} %bitcast.11, bf16[1,128,1024]{2,1,0:T(8,128)(2,1)S(1)} %collective-permute-done.17.refs_1_, bf16[1,128,1024]{2,1,0:T(8,128)(2,1)S(1)} %copy-done.9, bf16[1,128,1024]{2,1,0:T(8,128)(2,1)S(1)} %collective-permute-done.19.refs_3_, ...), custom_call_target="tpu_custom_call" | custom-call | flops 268435456 | bytes 894784 | tf_op jit(solution)/shard_map/pallas_call | solution.py:51
  98.1 1.5 %shard_map.123 = bf16[128,1024]{1,0:T(8,128)(2,1)} custom-call(bf16[64,1024]{1,0:T(8,128)(2,1)S(1)} %get-tuple-element.64.mine_ref, bf16[64,1024]{1,0:T(8,128)(2,1)S(1)} %collective-permute-done.26.pair_ref, bf16[1024,1024]{1,0:T(8,128)(2,1)S(1)} %copy-done.2), custom_call_target="tpu_custom_call" | custom-call | flops 268435456 | bytes 894784 | tf_op jit(solution)/shard_map/pallas_call | solution.py:51
  (95 shorter events, 20.7 us)
Async XLA Ops:
  0.6 40.0 %collective-permute-start.12 = (bf16[4,1024,512]{2,1,0:T(8,128)(2,1)}, bf16[4,1024,512]{2,1,0:T(8,128)(2,1)}, u32[]{:S(2)}, u32[]{:S(2)}) collective-permute-start(bf16[4,1024,512]{2,1,0:T(8,128)(2,1)} %head_mine.3), channel_id=1, source_target_pairs={{0,1},{1,0},{2,3},{3,2},{4,5},{5,4},{6,7},{7,6},{8,9},{9,8},{10,11... | collective-permute-start | bytes 12582920 | tf_op jit(solution)/shard_map/ppermute | solution.py:461
  1.2 26.7 %collective-permute-start.5 = (bf16[3,1024,256]{2,1,0:T(8,128)(2,1)}, bf16[3,1024,256]{2,1,0:T(8,128)(2,1)S(1)}, u32[]{:S(2)}, u32[]{:S(2)}) collective-permute-start(bf16[3,1024,256]{2,1,0:T(8,128)(2,1)} %bitcast.4), channel_id=1, source_target_pairs={{0,1},{1,0},{2,3},{3,2},{4,5},{5,4},{6,7},{7,6},{8,9},{9,8},{10,11... | collective-permute-start | bytes 4718600 | tf_op jit(solution)/shard_map/ppermute | solution.py:461
  2.4 11.1 %collective-permute-start.8 = (bf16[128,1024]{1,0:T(8,128)(2,1)S(1)}, bf16[128,1024]{1,0:T(8,128)(2,1)}, u32[]{:S(2)}, u32[]{:S(2)}) collective-permute-start(bf16[128,1024]{1,0:T(8,128)(2,1)S(1)} %shard_map.115), channel_id=1, source_target_pairs={{0,2},{1,3},{2,0},{3,1},{4,6},{5,7},{6,4},{7,5},{8,10},{9,11},{10,... | collective-permute-start | bytes 786440 | tf_op jit(solution)/shard_map/ppermute | solution.py:461
  11.1 6.6 %collective-permute-start = (bf16[64,1024]{1,0:T(8,128)(2,1)}, bf16[64,1024]{1,0:T(8,128)(2,1)S(1)}, u32[]{:S(2)}, u32[]{:S(2)}) collective-permute-start(bf16[64,1024]{1,0:T(8,128)(2,1)} %get-tuple-element.41), channel_id=1, source_target_pairs={{0,1},{1,0},{2,3},{3,2},{4,5},{5,4},{6,7},{7,6},{8,9},{9,8},{10,11... | collective-permute-start | bytes 393224 | tf_op jit(solution)/shard_map/ppermute | solution.py:461
  12.6 5.1 %collective-permute-start.3 = (bf16[3,64,256]{2,1,0:T(8,128)(2,1)}, bf16[3,64,256]{2,1,0:T(8,128)(2,1)S(1)}, u32[]{:S(2)}, u32[]{:S(2)}) collective-permute-start(bf16[3,64,256]{2,1,0:T(8,128)(2,1)} %get-tuple-element.42.look0), channel_id=1, source_target_pairs={{0,2},{1,3},{2,0},{3,1},{4,6},{5,7},{6,4},{7,5},{8,10},{9,11},{10,... | collective-permute-start | bytes 294920 | tf_op jit(solution)/shard_map/ppermute | solution.py:461
  13.4 14.0 %collective-permute-start.9 = (bf16[128,1024]{1,0:T(8,128)(2,1)}, bf16[128,1024]{1,0:T(8,128)(2,1)S(1)}, u32[]{:S(2)}, u32[]{:S(2)}) collective-permute-start(bf16[128,1024]{1,0:T(8,128)(2,1)} %collective-permute-done.8.part_a), channel_id=1, source_target_pairs={{0,4},{1,5},{2,6},{3,7},{4,0},{5,1},{6,2},{7,3},{8,12},{9,13},{10,... | collective-permute-start | bytes 786440 | tf_op jit(solution)/shard_map/ppermute | solution.py:469
  17.6 4.8 %collective-permute-start.4 = (bf16[3,64,256]{2,1,0:T(8,128)(2,1)}, bf16[3,64,256]{2,1,0:T(8,128)(2,1)S(1)}, u32[]{:S(2)}, u32[]{:S(2)}) collective-permute-start(bf16[3,64,256]{2,1,0:T(8,128)(2,1)} %get-tuple-element.43), channel_id=1, source_target_pairs={{0,3},{1,2},{2,1},{3,0},{4,7},{5,6},{6,5},{7,4},{8,11},{9,10},{10,... | collective-permute-start | bytes 294920 | tf_op jit(solution)/shard_map/ppermute | solution.py:461
  17.6 17.5 %collective-permute-start.7 = (bf16[256,1024]{1,0:T(8,128)(2,1)S(1)}, bf16[256,1024]{1,0:T(8,128)(2,1)S(1)}, u32[]{:S(2)}, u32[]{:S(2)}) collective-permute-start(bf16[256,1024]{1,0:T(8,128)(2,1)S(1)} %copy-done.4), channel_id=1, source_target_pairs={{0,1},{1,0},{2,3},{3,2},{4,5},{5,4},{6,7},{7,6},{8,9},{9,8},{10,11... | collective-permute-start | bytes 1572872 | tf_op jit(solution)/shard_map/ppermute | solution.py:461
  22.4 5.0 %collective-permute-start.1 = (bf16[64,1024]{1,0:T(8,128)(2,1)S(1)}, bf16[64,1024]{1,0:T(8,128)(2,1)S(1)}, u32[]{:S(2)}, u32[]{:S(2)}) collective-permute-start(bf16[64,1024]{1,0:T(8,128)(2,1)S(1)} %shard_map.113.own_ref), channel_id=1, source_target_pairs={{0,2},{1,3},{2,0},{3,1},{4,6},{5,7},{6,4},{7,5},{8,10},{9,11},{10,... | collective-permute-start | bytes 393224 | tf_op jit(solution)/shard_map/ppermute | solution.py:461
  27.4 6.1 %collective-permute-start.10 = (bf16[128,1024]{1,0:T(8,128)(2,1)}, bf16[128,1024]{1,0:T(8,128)(2,1)S(1)}, u32[]{:S(2)}, u32[]{:S(2)}) collective-permute-start(bf16[128,1024]{1,0:T(8,128)(2,1)} %collective-permute-done.8.part_a), channel_id=1, source_target_pairs={{0,1},{1,0},{2,3},{3,2},{4,5},{5,4},{6,7},{7,6},{8,9},{9,8},{10,11... | collective-permute-start | bytes 786440 | tf_op jit(solution)/shard_map/ppermute | solution.py:461
  27.4 10.3 %collective-permute-start.11 = (bf16[128,1024]{1,0:T(8,128)(2,1)S(1)}, bf16[128,1024]{1,0:T(8,128)(2,1)S(1)}, u32[]{:S(2)}, u32[]{:S(2)}) collective-permute-start(bf16[128,1024]{1,0:T(8,128)(2,1)S(1)} %collective-permute-done.9.part_b), channel_id=1, source_target_pairs={{0,1},{1,0},{2,3},{3,2},{4,5},{5,4},{6,7},{7,6},{8,9},{9,8},{10,11... | collective-permute-start | bytes 786440 | tf_op jit(solution)/shard_map/ppermute | solution.py:461
  32.1 8.5 %collective-permute-start.6 = (bf16[256,512]{1,0:T(8,128)(2,1)S(1)}, bf16[256,512]{1,0:T(8,128)(2,1)S(1)}, u32[]{:S(2)}, u32[]{:S(2)}) collective-permute-start(bf16[256,512]{1,0:T(8,128)(2,1)S(1)} %get-tuple-element.44.att_ref), channel_id=1, source_target_pairs={{0,2},{1,3},{2,0},{3,1},{4,6},{5,7},{6,4},{7,5},{8,10},{9,11},{10,... | collective-permute-start | bytes 786440 | tf_op jit(solution)/shard_map/ppermute | solution.py:461
  33.5 23.9 %collective-permute-start.18 = (bf16[1,128,1024]{2,1,0:T(8,128)(2,1)S(1)}, bf16[1,128,1024]{2,1,0:T(8,128)(2,1)S(1)}, u32[]{:S(2)}, u32[]{:S(2)}) collective-permute-start(bf16[1,128,1024]{2,1,0:T(8,128)(2,1)S(1)} %bitcast.7), channel_id=1, source_target_pairs={{0,8},{1,9},{2,10},{3,11},{4,12},{5,13},{6,14},{7,15},{8,16},{9,17... | collective-permute-start | bytes 786440 | tf_op jit(solution)/shard_map/ppermute | solution.py:469
  35.1 22.8 %collective-permute-start.20 = (bf16[1,128,1024]{2,1,0:T(8,128)(2,1)S(1)}, bf16[1,128,1024]{2,1,0:T(8,128)(2,1)S(1)}, u32[]{:S(2)}, u32[]{:S(2)}) collective-permute-start(bf16[1,128,1024]{2,1,0:T(8,128)(2,1)S(1)} %bitcast.8), channel_id=1, source_target_pairs={{0,16},{1,17},{2,18},{3,19},{4,20},{5,21},{6,22},{7,23},{8,24},{9,... | collective-permute-start | bytes 786440 | tf_op jit(solution)/shard_map/ppermute | solution.py:469
  37.7 20.2 %collective-permute-start.22 = (bf16[1,128,1024]{2,1,0:T(8,128)(2,1)S(1)}, bf16[1,128,1024]{2,1,0:T(8,128)(2,1)S(1)}, u32[]{:S(2)}, u32[]{:S(2)}) collective-permute-start(bf16[1,128,1024]{2,1,0:T(8,128)(2,1)S(1)} %bitcast.9), channel_id=1, source_target_pairs={{0,24},{1,25},{2,26},{3,27},{4,28},{5,29},{6,30},{7,31},{8,0},{9,1... | collective-permute-start | bytes 786440 | tf_op jit(solution)/shard_map/ppermute | solution.py:469
  46.4 6.2 %collective-permute-start.13 = (f32[64,128]{1,0:T(8,128)S(1)}, f32[64,128]{1,0:T(8,128)S(1)}, u32[]{:S(2)}, u32[]{:S(2)}) collective-permute-start(f32[64,128]{1,0:T(8,128)S(1)} %get-tuple-element.50.stats_ref), channel_id=1, source_target_pairs={{0,2},{1,3},{2,0},{3,1},{4,6},{5,7},{6,4},{7,5},{8,10},{9,11},{10,... | collective-permute-start | bytes 98312 | tf_op jit(solution)/shard_map/ppermute | solution.py:461
  54.9 7.2 %collective-permute-start.15 = (bf16[256,512]{1,0:T(8,128)(2,1)S(1)}, bf16[256,512]{1,0:T(8,128)(2,1)S(1)}, u32[]{:S(2)}, u32[]{:S(2)}) collective-permute-start(bf16[256,512]{1,0:T(8,128)(2,1)S(1)} %get-tuple-element.55), channel_id=1, source_target_pairs={{0,2},{1,3},{2,0},{3,1},{4,6},{5,7},{6,4},{7,5},{8,10},{9,11},{10,... | collective-permute-start | bytes 786440 | tf_op jit(solution)/shard_map/ppermute | solution.py:461
  55.9 10.1 %collective-permute-start.17 = (bf16[1,128,1024]{2,1,0:T(8,128)(2,1)S(1)}, bf16[1,128,1024]{2,1,0:T(8,128)(2,1)S(1)}, u32[]{:S(2)}, u32[]{:S(2)}) collective-permute-start(bf16[1,128,1024]{2,1,0:T(8,128)(2,1)S(1)} %bitcast.10), channel_id=1, source_target_pairs={{0,4},{1,5},{2,6},{3,7},{4,0},{5,1},{6,2},{7,3},{8,12},{9,13},{10,... | collective-permute-start | bytes 786440 | tf_op jit(solution)/shard_map/ppermute | solution.py:469
  57.4 14.0 %collective-permute-start.19 = (bf16[1,128,1024]{2,1,0:T(8,128)(2,1)S(1)}, bf16[1,128,1024]{2,1,0:T(8,128)(2,1)S(1)}, u32[]{:S(2)}, u32[]{:S(2)}) collective-permute-start(bf16[1,128,1024]{2,1,0:T(8,128)(2,1)S(1)} %collective-permute-done.18.refs_2_), channel_id=1, source_target_pairs={{0,4},{1,5},{2,6},{3,7},{4,0},{5,1},{6,2},{7,3},{8,12},{9,13},{10,... | collective-permute-start | bytes 786440 | tf_op jit(solution)/shard_map/ppermute | solution.py:469
  57.9 1.6 %collective-permute-start.14 = (f32[64,4]{1,0:T(8,128)S(1)}, f32[64,4]{1,0:T(8,128)S(1)}, u32[]{:S(2)}, u32[]{:S(2)}) collective-permute-start(f32[64,4]{1,0:T(8,128)S(1)} %get-tuple-element.52.loss_mine), channel_id=1, source_target_pairs={{0,1},{1,0},{2,3},{3,2},{4,5},{5,4},{6,7},{7,6},{8,9},{9,8},{10,11... | collective-permute-start | bytes 3080 | tf_op jit(solution)/shard_map/ppermute | solution.py:461
  57.9 19.8 %collective-permute-start.21 = (bf16[1,128,1024]{2,1,0:T(8,128)(2,1)S(1)}, bf16[1,128,1024]{2,1,0:T(8,128)(2,1)S(1)}, u32[]{:S(2)}, u32[]{:S(2)}) collective-permute-start(bf16[1,128,1024]{2,1,0:T(8,128)(2,1)S(1)} %collective-permute-done.20.refs_4_), channel_id=1, source_target_pairs={{0,4},{1,5},{2,6},{3,7},{4,0},{5,1},{6,2},{7,3},{8,12},{9,13},{10,... | collective-permute-start | bytes 786440 | tf_op jit(solution)/shard_map/ppermute | solution.py:469
  59.5 21.9 %collective-permute-start.23 = (bf16[1,128,1024]{2,1,0:T(8,128)(2,1)S(1)}, bf16[1,128,1024]{2,1,0:T(8,128)(2,1)S(1)}, u32[]{:S(2)}, u32[]{:S(2)}) collective-permute-start(bf16[1,128,1024]{2,1,0:T(8,128)(2,1)S(1)} %collective-permute-done.22.refs_6_), channel_id=1, source_target_pairs={{0,4},{1,5},{2,6},{3,7},{4,0},{5,1},{6,2},{7,3},{8,12},{9,13},{10,... | collective-permute-start | bytes 786440 | tf_op jit(solution)/shard_map/ppermute | solution.py:469
  65.3 16.8 %collective-permute-start.16 = (bf16[64,1024]{1,0:T(8,128)(2,1)S(1)}, bf16[64,1024]{1,0:T(8,128)(2,1)S(1)}, u32[]{:S(2)}, u32[]{:S(2)}) collective-permute-start(bf16[64,1024]{1,0:T(8,128)(2,1)S(1)} %get-tuple-element.61.refs_0_), channel_id=1, source_target_pairs={{0,2},{1,3},{2,0},{3,1},{4,6},{5,7},{6,4},{7,5},{8,10},{9,11},{10,... | collective-permute-start | bytes 393224 | tf_op jit(solution)/shard_map/ppermute | solution.py:461
  66.0 16.1 %collective-permute-start.24 = (bf16[4,64,128]{2,1,0:T(8,128)(2,1)S(1)}, bf16[4,64,128]{2,1,0:T(8,128)(2,1)S(1)}, u32[]{:S(2)}, u32[]{:S(2)}) collective-permute-start(bf16[4,64,128]{2,1,0:T(8,128)(2,1)S(1)} %get-tuple-element.63), channel_id=1, source_target_pairs={{0,4},{1,5},{2,6},{3,7},{4,0},{5,1},{6,2},{7,3},{8,12},{9,13},{10,... | collective-permute-start | bytes 196616 | tf_op jit(solution)/shard_map/ppermute | solution.py:469
  71.4 10.8 %collective-permute-start.25 = (bf16[4,64,128]{2,1,0:T(8,128)(2,1)S(1)}, bf16[4,64,128]{2,1,0:T(8,128)(2,1)S(1)}, u32[]{:S(2)}, u32[]{:S(2)}) collective-permute-start(bf16[4,64,128]{2,1,0:T(8,128)(2,1)S(1)} %get-tuple-element.63), channel_id=1, source_target_pairs={{0,6},{1,7},{2,4},{3,5},{4,2},{5,3},{6,0},{7,1},{8,14},{9,15},{10,... | collective-permute-start | bytes 196616 | tf_op jit(solution)/shard_map/ppermute | solution.py:469
  82.2 15.9 %collective-permute-start.26 = (bf16[64,1024]{1,0:T(8,128)(2,1)S(1)}, bf16[64,1024]{1,0:T(8,128)(2,1)S(1)}, u32[]{:S(2)}, u32[]{:S(2)}) collective-permute-start(bf16[64,1024]{1,0:T(8,128)(2,1)S(1)} %get-tuple-element.64.mine_ref), channel_id=1, source_target_pairs={{0,1},{1,0},{2,3},{3,2},{4,5},{5,4},{6,7},{7,6},{8,9},{9,8},{10,11... | collective-permute-start | bytes 393224 | tf_op jit(solution)/shard_map/ppermute | solution.py:461
  82.3 5.8 %collective-permute-start.27 = (bf16[2,1,64,128]{3,2,1,0:T(8,128)(2,1)S(1)}, bf16[2,1,64,128]{3,2,1,0:T(8,128)(2,1)S(1)}, u32[]{:S(2)}, u32[]{:S(2)}) collective-permute-start(bf16[2,1,64,128]{3,2,1,0:T(8,128)(2,1)S(1)} %get-tuple-element.74), channel_id=1, source_target_pairs={{0,8},{1,9},{2,10},{3,11},{4,12},{5,13},{6,14},{7,15},{8,16},{9,17... | collective-permute-start | bytes 98312 | tf_op jit(solution)/shard_map/ppermute | solution.py:469
  83.9 5.2 %collective-permute-start.28 = (bf16[2,1,64,128]{3,2,1,0:T(8,128)(2,1)S(1)}, bf16[2,1,64,128]{3,2,1,0:T(8,128)(2,1)S(1)}, u32[]{:S(2)}, u32[]{:S(2)}) collective-permute-start(bf16[2,1,64,128]{3,2,1,0:T(8,128)(2,1)S(1)} %get-tuple-element.75), channel_id=1, source_target_pairs={{0,16},{1,17},{2,18},{3,19},{4,20},{5,21},{6,22},{7,23},{8,24},{9,... | collective-permute-start | bytes 98312 | tf_op jit(solution)/shard_map/ppermute | solution.py:469
  86.5 3.9 %collective-permute-start.29 = (bf16[2,1,64,128]{3,2,1,0:T(8,128)(2,1)S(1)}, bf16[2,1,64,128]{3,2,1,0:T(8,128)(2,1)S(1)}, u32[]{:S(2)}, u32[]{:S(2)}) collective-permute-start(bf16[2,1,64,128]{3,2,1,0:T(8,128)(2,1)S(1)} %get-tuple-element.76), channel_id=1, source_target_pairs={{0,24},{1,25},{2,26},{3,27},{4,28},{5,29},{6,30},{7,31},{8,0},{9,1... | collective-permute-start | bytes 98312 | tf_op jit(solution)/shard_map/ppermute | solution.py:469
  87.9 3.2 %collective-permute-start.30 = (bf16[2,1,64,128]{3,2,1,0:T(8,128)(2,1)S(1)}, bf16[2,1,64,128]{3,2,1,0:T(8,128)(2,1)S(1)}, u32[]{:S(2)}, u32[]{:S(2)}) collective-permute-start(bf16[2,1,64,128]{3,2,1,0:T(8,128)(2,1)S(1)} %get-tuple-element.73.refs_8_), channel_id=1, source_target_pairs={{0,1},{1,0},{2,3},{3,2},{4,5},{5,4},{6,7},{7,6},{8,9},{9,8},{10,11... | collective-permute-start | bytes 98312 | tf_op jit(solution)/shard_map/ppermute | solution.py:461
  88.1 3.0 %collective-permute-start.31 = (bf16[2,1,64,128]{3,2,1,0:T(8,128)(2,1)S(1)}, bf16[2,1,64,128]{3,2,1,0:T(8,128)(2,1)S(1)}, u32[]{:S(2)}, u32[]{:S(2)}) collective-permute-start(bf16[2,1,64,128]{3,2,1,0:T(8,128)(2,1)S(1)} %collective-permute-done.27.refs_9_), channel_id=1, source_target_pairs={{0,1},{1,0},{2,3},{3,2},{4,5},{5,4},{6,7},{7,6},{8,9},{9,8},{10,11... | collective-permute-start | bytes 98312 | tf_op jit(solution)/shard_map/ppermute | solution.py:461
  89.2 2.0 %collective-permute-start.32 = (bf16[2,1,64,128]{3,2,1,0:T(8,128)(2,1)S(1)}, bf16[2,1,64,128]{3,2,1,0:T(8,128)(2,1)S(1)}, u32[]{:S(2)}, u32[]{:S(2)}) collective-permute-start(bf16[2,1,64,128]{3,2,1,0:T(8,128)(2,1)S(1)} %collective-permute-done.28.refs_10_), channel_id=1, source_target_pairs={{0,1},{1,0},{2,3},{3,2},{4,5},{5,4},{6,7},{7,6},{8,9},{9,8},{10,11... | collective-permute-start | bytes 98312 | tf_op jit(solution)/shard_map/ppermute | solution.py:461
  (24 other events, 168.4 us)

commit v2 on v1

--- a/solution.py
+++ b/solution.py
@@ -75,28 +75,30 @@
     copy.wait()
 
 
-def enter_kernel(
-    hidden_ref, weight_ref, codes_ref, table_hbm, mine_ref, other_ref, look_mine, look_other, table_ref, sems,
-):
-    count, half = look_mine.shape[:2]
+def context_kernel(hidden_ref, weight_ref, mine_ref, other_ref):
+    half = mine_ref.shape[0]
+    core = lax.axis_index("tp") % 2
+    low = hidden_ref[pl.ds(pl.multiple_of(core * half, half), half), :]
+    high = hidden_ref[pl.ds(pl.multiple_of((1 - core) * half, half), half), :]
+    partial = dot(jnp.concatenate([low, high], axis=0), weight_ref[...])
+    mine_ref[...] = partial[:half]
+    other_ref[...] = partial[half:].astype(BF16)
+
+
+def lookup_kernel(codes_ref, table_ref, mine_ref, other_ref, code_ref):
+    count, half = mine_ref.shape[:2]
     vocab = table_ref.shape[1]
     core = lax.axis_index("tp") % 2
-    copies = [pltpu.make_async_copy(table_hbm.at[k], table_ref.at[k], sems.at[k]) for k in range(count)]
-    for copy in copies:
-        copy.start()
-    low = pl.ds(pl.multiple_of(core * half, half), half)
-    high = pl.ds(pl.multiple_of((1 - core) * half, half), half)
-    partial = dot(jnp.concatenate([hidden_ref[low, :], hidden_ref[high, :]], axis=0), weight_ref[...])
-    mine_ref[...] = partial[:half]
-    other_ref[...] = partial[half:].astype(BF16)
-    codes = jnp.concatenate([codes_ref[low, :], codes_ref[high, :]], axis=0)
+    code_ref[...] = codes_ref[...].T
+    low = code_ref[pl.ds(pl.multiple_of(core * half, half), half), :]
+    high = code_ref[pl.ds(pl.multiple_of((1 - core) * half, half), half), :]
+    codes = jnp.concatenate([low, high], axis=0)
     lanes = lax.broadcasted_iota(jnp.int32, (2 * half, vocab), 1)
     for k in range(count):
         chosen = jnp.where(lanes == codes[:, k : k + 1], 1.0, 0.0).astype(BF16)
-        copies[k].wait()
         found = dot(chosen, table_ref[k]).astype(BF16)
-        look_mine[k] = found[:half]
-        look_other[k] = found[half:]
+        mine_ref[k] = found[:half]
+        other_ref[k] = found[half:]
 
 
 def join_kernel(mine_ref, other_ref, out_ref):
@@ -185,9 +187,10 @@
 
 def head_kernel(
     att_theirs, full_ref, stream_ref, gain_ref, codes_ref, head_mine, head_pair,
-    mid_ref, expo_ref, stats_ref, mixed_ref, normed_ref, logit_ref,
+    mid_ref, expo_ref, stats_ref, mixed_ref, normed_ref, logit_ref, code_ref,
 ):
     steps, half, _ = stream_ref.shape
+    code_ref[...] = codes_ref[...].T
     rank = lax.axis_index("tp")
     core = rank % 2
     vocab = head_mine.shape[2]
@@ -214,7 +217,7 @@
         ids = jnp.where(lanes < vocab, lanes + rank * vocab, lanes - vocab + (rank ^ 1) * vocab)
         spots = lax.broadcasted_iota(jnp.int32, (ROWS, stats_ref.shape[1]), 1)
         stats = jnp.zeros((ROWS, stats_ref.shape[1]), F32)
-        codes = codes_ref[pl.ds(pl.multiple_of(core * half + i * ROWS, ROWS), ROWS), :]
+        codes = code_ref[pl.ds(pl.multiple_of(core * half + i * ROWS, ROWS), ROWS), :]
         for k in range(steps):
             logits = logit_ref[k, chunk(i), :]
             hits = ids == codes[:, k : k + 1]
@@ -249,8 +252,8 @@
     def leave(i, carry):
         mine = stats_ref[chunk(i), :]
         theirs = stats_side[chunk(i), :]
-        spots = lax.broadcasted_iota(jnp.int32, (ROWS, steps), 1)
-        losses = jnp.zeros((ROWS, steps), F32)
+        spots = lax.broadcasted_iota(jnp.int32, loss_ref[chunk(i), :].shape, 1)
+        losses = jnp.zeros(spots.shape, F32)
         added = 0.0
         for k in range(steps):
             top_a, sum_a, target_a = [mine[:, 3 * k + j : 3 * k + j + 1] for j in range(3)]
@@ -274,11 +277,12 @@
     send_ref[...] = dot_t(low_ref[...], out_ref[middle : 2 * middle, :]).astype(BF16)
 
 
-def keep_kernel(low_ref, out_ref, loss_mine, loss_pair, keep_ref, loss_ref):
+def keep_kernel(low_ref, out_ref, loss_mine, loss_pair, keep_ref, loss_ref, full_ref):
     half = loss_mine.shape[0]
     core = lax.axis_index("tp") % 2
-    loss_ref[pl.ds(pl.multiple_of(core * half, half), half), :] = loss_mine[...]
-    loss_ref[pl.ds(pl.multiple_of((1 - core) * half, half), half), :] = loss_pair[...]
+    full_ref[pl.ds(pl.multiple_of(core * half, half), half), :] = loss_mine[...]
+    full_ref[pl.ds(pl.multiple_of((1 - core) * half, half), half), :] = loss_pair[...]
+    loss_ref[...] = full_ref[...].T[: loss_ref.shape[0], :]
     keep_ref[...] = dot_t(low_ref[...], out_ref[0 : out_ref.shape[0] // 2, :])
 
 
@@ -473,11 +477,14 @@
         cut_kernel, [((cut, width), BF16)], [pltpu.SemaphoreType.DMA], (w_out,), 6 * 10**9, {0: pltpu.HBM}, limit=4
     )
     out_part = to_peer(out_part, 2)
-    partial, partial_other, looked, looked_other = call(
-        enter_kernel,
-        [((half, width), F32), ((half, width), BF16)] + [((steps - 1, half, lanes), BF16)] * 2,
-        [pltpu.VMEM(embed_table.shape, BF16), pltpu.SemaphoreType.DMA((steps - 1,))],
-        (hidden, w_proj, codes, embed_table), 6 * 10**9, {3: pltpu.HBM}, limit=60,
+    partial, partial_other = call(
+        context_kernel, [((half, width), F32), ((half, width), BF16)], [],
+        (hidden, w_proj), 6 * 10**9, limit=8,
+    )
+    looked, looked_other = call(
+        lookup_kernel, [((steps - 1, half, lanes), BF16)] * 2,
+        [pltpu.VMEM((frames, steps), jnp.int32)],
+        (codes.T, embed_table), 6 * 10**9, limit=8,
     )
     (partial,) = call(
         join_kernel, [((half, width), BF16)], [],
@@ -532,8 +539,9 @@
             pltpu.VMEM((rows, width), F32),
             pltpu.VMEM((rows, width), BF16),
             pltpu.VMEM((steps, half, 2 * vocab_local), F32),
+            pltpu.VMEM((frames, steps), jnp.int32),
         ],
-        (att_theirs, out_full, mixed, gain_head, codes, head_table, head_pair),
+        (att_theirs, out_full, mixed, gain_head, codes.T, head_table, head_pair),
         4 * half * head_table.size + rows * width * width,
     )
     stats_side = to_peer(stats, 2)
@@ -543,12 +551,12 @@
     )
     att_send, mid_low, mid_sum, losses = call(
         functools.partial(mid_kernel, total),
-        [((rows, 2 * lanes), BF16), ((rows, width), BF16), ((half, width), F32), ((half, steps), F32)],
+        [((rows, 2 * lanes), BF16), ((rows, width), BF16), ((half, width), F32), ((half, 128), F32)],
         [], (both, stream_mid, gain_head, stats, stats_side, out_full), rows * width * width,
     )
     att_recv = to_peer(att_send, 2)
     att_keep, row_loss = call(
-        keep_kernel, [((rows, 2 * lanes), F32), ((frames, steps), F32)], [],
+        keep_kernel, [((rows, 2 * lanes), F32), ((steps, frames), F32)], [pltpu.VMEM((frames, 128), F32)],
         (mid_low, out_full, losses, to_peer(losses, 1)), rows * width * width,
     )
     size = width // seq
@@ -604,7 +612,7 @@
         [pltpu.VMEM((seq, frames, size), BF16)],
         (*states, *owned, *paired), 2 * frames * seq * hidden.shape[1] * size, limit=40 if seq > 16 else 12,
     )
-    return (row_loss, grad_hidden, grad_proj)
+    return (row_loss.T, grad_hidden, grad_proj)
 
 
 def solution(mesh):

time: 100 us -> 90 us (0.900)
  Pallas kernels: 29.7 us -> 21.1 us
  local copies, waits for them, and re-layouts: 10.5 us -> 2.62 us
  starting transfers between devices: 33.2 us -> 37.3 us
  waiting for transfers between devices: 25.3 us -> 28 us
    pallas_call x13 -> x14, Pallas kernels: 29.7 us -> 21.1 us  [call(): pl.pallas_call(kernel, out_shape=[jax.ShapeDtypeStruct(shape, dtype) for...]
    unnamed x46 -> x20, local copies, waits for them, and re-layouts: 10.5 us -> 2.62 us
    ppermute x21, starting transfers between devices: 12.3 us -> 16.4 us  [to_peer(): return lax.ppermute(value, 'tp', [(i, i ^ flip) for i in range(tp)])]
    ppermute x13, waiting for transfers between devices: 13.4 us -> 15.3 us  [along(): return lax.ppermute(value, ('seq', 'tp'), route)]
  transfers between devices with their start and end apart: 34 -> 34, of which waited for: 12 -> 14; matrix products, arithmetic and copies ran while one was open for 1% -> 0% of each run, Pallas kernels for 28% -> 22%
where the time goes in v2:
time: 90 us; the launch traced here: 89.9 us
  starting transfers between devices  37.3 us (41%)
  waiting for transfers between devices  28 us (31%)
  Pallas kernels  21.1 us (23%)
  local copies, waits for them, and re-layouts  2.62 us (3%)
    pallas_call x14, Pallas kernels, call(): pl.pallas_call(kernel, out_shape=[jax.ShapeDtypeStruct(shape, dtype) for...  21.1 us
    ppermute x13, starting transfers between devices, along(): return lax.ppermute(value, ('seq', 'tp'), route)  20.9 us
    ppermute x21, starting transfers between devices, to_peer(): return lax.ppermute(value, 'tp', [(i, i ^ flip) for i in range(tp)])  16.4 us
    ppermute x13, waiting for transfers between devices, along(): return lax.ppermute(value, ('seq', 'tp'), route)  15.3 us
    ppermute x21, waiting for transfers between devices, to_peer(): return lax.ppermute(value, 'tp', [(i, i ^ flip) for i in range(tp)])  12.7 us
    unnamed x20, local copies, waits for them, and re-layouts  2.62 us
  transfers between devices with their start and end apart: 34, of which 14 were waited for; matrix products, arithmetic and copies ran while one was open for 0% of the time, Pallas kernels for 22%

profile of v2, /device:TPU:0, one launch (start us, length us, event | category | flops | bytes accessed | tf_op | source)
XLA Modules:
  0.0 89.9 jit_solution(3474986239276026143)
XLA Ops:
  2.0 1.9 %copy-done.9 = bf16[3,2048,256]{2,1,0:T(8,128)(2,1)S(1)} copy-done((bf16[3,2048,256]{2,1,0:T(8,128)(2,1)S(1)}, bf16[3,2048,256]{2,1,0:T(8,128)(2,1)}, u32[]{:S(2)}) %copy-start.9) | copy-done | bytes 3145752
  5.2 2.7 %collective-permute-start.8 = (bf16[128,1024]{1,0:T(8,128)(2,1)S(1)}, bf16[128,1024]{1,0:T(8,128)(2,1)S(1)}, u32[]{:S(2)}, u32[]{:S(2)}) collective-permute-start(bf16[128,1024]{1,0:T(8,128)(2,1)S(1)} %shard_map.116), channel_id=1, source_target_pairs={{0,2},{1,3},{2,0},{3,1},{4,6},{5,7},{6,4},{7,5},{8,10},{9,11},{10,... | collective-permute-start | bytes 786440 | tf_op jit(solution)/shard_map/ppermute | solution.py:465
  8.5 2.1 %collective-permute-done.2.look1 = bf16[3,64,256]{2,1,0:T(8,128)(2,1)S(1)} collective-permute-done((bf16[3,64,256]{2,1,0:T(8,128)(2,1)S(1)}, bf16[3,64,256]{2,1,0:T(8,128)(2,1)S(1)}, u32[]{:S(2)}, u32[]{:S(2)}) %collective-permute-start.2) | collective-permute-done | bytes 98336 | tf_op jit(solution)/shard_map/ppermute | solution.py:465
  10.6 2.8 %collective-permute-start.3 = (bf16[3,64,256]{2,1,0:T(8,128)(2,1)S(1)}, bf16[3,64,256]{2,1,0:T(8,128)(2,1)S(1)}, u32[]{:S(2)}, u32[]{:S(2)}) collective-permute-start(bf16[3,64,256]{2,1,0:T(8,128)(2,1)S(1)} %get-tuple-element.42.look0), channel_id=1, source_target_pairs={{0,2},{1,3},{2,0},{3,1},{4,6},{5,7},{6,4},{7,5},{8,10},{9,11},{10,... | collective-permute-start | bytes 294920 | tf_op jit(solution)/shard_map/ppermute | solution.py:465
  13.4 1.6 %collective-permute-done.8.part_a = bf16[128,1024]{1,0:T(8,128)(2,1)S(1)} collective-permute-done((bf16[128,1024]{1,0:T(8,128)(2,1)S(1)}, bf16[128,1024]{1,0:T(8,128)(2,1)S(1)}, u32[]{:S(2)}, u32[]{:S(2)}) %collective-permute-start.8) | collective-permute-done | bytes 262176 | tf_op jit(solution)/shard_map/ppermute | solution.py:465
  15.0 1.8 %collective-permute-start.9 = (bf16[128,1024]{1,0:T(8,128)(2,1)S(1)}, bf16[128,1024]{1,0:T(8,128)(2,1)S(1)}, u32[]{:S(2)}, u32[]{:S(2)}) collective-permute-start(bf16[128,1024]{1,0:T(8,128)(2,1)S(1)} %collective-permute-done.8.part_a), channel_id=1, source_target_pairs={{0,4},{1,5},{2,6},{3,7},{4,0},{5,1},{6,2},{7,3},{8,12},{9,13},{10,... | collective-permute-start | bytes 786440 | tf_op jit(solution)/shard_map/ppermute | solution.py:473
  18.7 2.9 %collective-permute-done.4.look3 = bf16[3,64,256]{2,1,0:T(8,128)(2,1)S(1)} collective-permute-done((bf16[3,64,256]{2,1,0:T(8,128)(2,1)S(1)}, bf16[3,64,256]{2,1,0:T(8,128)(2,1)S(1)}, u32[]{:S(2)}, u32[]{:S(2)}) %collective-permute-start.4) | collective-permute-done | bytes 98336 | tf_op jit(solution)/shard_map/ppermute | solution.py:465
  21.6 1.8 %collective-permute-start.1 = (bf16[64,1024]{1,0:T(8,128)(2,1)S(1)}, bf16[64,1024]{1,0:T(8,128)(2,1)S(1)}, u32[]{:S(2)}, u32[]{:S(2)}) collective-permute-start(bf16[64,1024]{1,0:T(8,128)(2,1)S(1)} %shard_map.113.own_ref), channel_id=1, source_target_pairs={{0,2},{1,3},{2,0},{3,1},{4,6},{5,7},{6,4},{7,5},{8,10},{9,11},{10,... | collective-permute-start | bytes 393224 | tf_op jit(solution)/shard_map/ppermute | solution.py:465
  23.4 4.0 %collective-permute-done.1.side_ref = bf16[64,1024]{1,0:T(8,128)(2,1)S(1)} collective-permute-done((bf16[64,1024]{1,0:T(8,128)(2,1)S(1)}, bf16[64,1024]{1,0:T(8,128)(2,1)S(1)}, u32[]{:S(2)}, u32[]{:S(2)}) %collective-permute-start.1) | collective-permute-done | bytes 131104 | tf_op jit(solution)/shard_map/ppermute | solution.py:465
  28.0 3.3 %shard_map.115 = (f32[4,64,1024]{2,1,0:T(8,128)S(1)}, bf16[256,512]{1,0:T(8,128)(2,1)S(1)}, bf16[256,768]{1,0:T(8,128)(2,1)S(1)}, bf16[256,768]{1,0:T(8,128)(2,1...) custom-call(bf16[64,1024]{1,0:T(8,128)(2,1)S(1)} %shard_map.113.own_ref, ...), custom_call_target="tpu_custom_call" | custom-call | flops 805306368 | bytes 2684354 | tf_op jit(solution)/shard_map/pallas_call | solution.py:51
  31.3 1.3 %collective-permute-start.6 = (bf16[256,512]{1,0:T(8,128)(2,1)S(1)}, bf16[256,512]{1,0:T(8,128)(2,1)S(1)}, u32[]{:S(2)}, u32[]{:S(2)}) collective-permute-start(bf16[256,512]{1,0:T(8,128)(2,1)S(1)} %get-tuple-element.44.att_ref), channel_id=1, source_target_pairs={{0,2},{1,3},{2,0},{3,1},{4,6},{5,7},{6,4},{7,5},{8,10},{9,11},{10,... | collective-permute-start | bytes 786440 | tf_op jit(solution)/shard_map/ppermute | solution.py:465
  32.7 1.6 %collective-permute-start.18 = (bf16[1,128,1024]{2,1,0:T(8,128)(2,1)S(1)}, bf16[1,128,1024]{2,1,0:T(8,128)(2,1)S(1)}, u32[]{:S(2)}, u32[]{:S(2)}) collective-permute-start(bf16[1,128,1024]{2,1,0:T(8,128)(2,1)S(1)} %bitcast.9), channel_id=1, source_target_pairs={{0,8},{1,9},{2,10},{3,11},{4,12},{5,13},{6,14},{7,15},{8,16},{9,17... | collective-permute-start | bytes 786440 | tf_op jit(solution)/shard_map/ppermute | solution.py:473
  34.2 2.6 %collective-permute-start.20 = (bf16[1,128,1024]{2,1,0:T(8,128)(2,1)S(1)}, bf16[1,128,1024]{2,1,0:T(8,128)(2,1)S(1)}, u32[]{:S(2)}, u32[]{:S(2)}) collective-permute-start(bf16[1,128,1024]{2,1,0:T(8,128)(2,1)S(1)} %bitcast.10), channel_id=1, source_target_pairs={{0,16},{1,17},{2,18},{3,19},{4,20},{5,21},{6,22},{7,23},{8,24},{9,... | collective-permute-start | bytes 786440 | tf_op jit(solution)/shard_map/ppermute | solution.py:473
  36.8 1.4 %collective-permute-start.22 = (bf16[1,128,1024]{2,1,0:T(8,128)(2,1)S(1)}, bf16[1,128,1024]{2,1,0:T(8,128)(2,1)S(1)}, u32[]{:S(2)}, u32[]{:S(2)}) collective-permute-start(bf16[1,128,1024]{2,1,0:T(8,128)(2,1)S(1)} %bitcast.11), channel_id=1, source_target_pairs={{0,24},{1,25},{2,26},{3,27},{4,28},{5,29},{6,30},{7,31},{8,0},{9,1... | collective-permute-start | bytes 786440 | tf_op jit(solution)/shard_map/ppermute | solution.py:473
  39.6 3.5 %shard_map.118 = (f32[4,64,1024]{2,1,0:T(8,128)S(1)}, bf16[4,128,1024]{2,1,0:T(8,128)(2,1)S(1)}, f32[64,128]{1,0:T(8,128)S(1)}) custom-call(bf16[256,512]{1,0:T(8,128)(2,1)S(1)} %collective-permute-done.6.att_theirs, bf16[1024,1024]{1,0:T(8,128)(2,1)S(1)} %get-tuple-element.46.full_ref.out_ref, f32[4,64,1024]{2,1,0:T(8,128)S(1)} %get-tuple-element.47.stream_ref, ...), custom_call_target="tpu_custom_call" | custom-call | flops 805306368 | bytes 2684354 | tf_op jit(solution)/shard_map/pallas_call | solution.py:51
  43.1 1.4 %collective-permute-start.13 = (f32[64,128]{1,0:T(8,128)S(1)}, f32[64,128]{1,0:T(8,128)S(1)}, u32[]{:S(2)}, u32[]{:S(2)}) collective-permute-start(f32[64,128]{1,0:T(8,128)S(1)} %get-tuple-element.50.stats_ref), channel_id=1, source_target_pairs={{0,2},{1,3},{2,0},{3,1},{4,6},{5,7},{6,4},{7,5},{8,10},{9,11},{10,... | collective-permute-start | bytes 98312 | tf_op jit(solution)/shard_map/ppermute | solution.py:465
  44.5 2.8 %shard_map.119.both_ref = f32[4,128,1024]{2,1,0:T(8,128)S(1)} custom-call(bf16[4,128,1024]{2,1,0:T(8,128)(2,1)S(1)} %get-tuple-element.48.expo_ref, bf16[4,1024,512]{2,1,0:T(8,128)(2,1)S(1)} %copy-done, bf16[4,1024,512]{2,1,0:T(8,128)(2,1)S(1)} %collective-permute-done.12.head_pair), custom_call_target="tpu_custom_call" | custom-call | flops 1073741824 | bytes 3579139 | tf_op jit(solution)/shard_map/pallas_call | solution.py:51
  47.3 2.3 %shard_map.120 = (bf16[256,512]{1,0:T(8,128)(2,1)S(1)}, bf16[256,1024]{1,0:T(8,128)(2,1)S(1)}, f32[64,1024]{1,0:T(8,128)S(1)}, f32[64,128]{1,0:T(8,128)S(1)}) custom-call(f32[4,128,1024]{2,1,0:T(8,128)S(1)} %shard_map.119.both_ref, f32[4,64,1024]{2,1,0:T(8,128)S(1)} %get-tuple-element.49.mid_ref, f32[1,1024]{1,0:T(1,128)S(1)} %bitcast.15, ...), custom_call_target="tpu_custom_call" | custom-call | flops 268435456 | bytes 894784 | tf_op jit(solution)/shard_map/pallas_call | solution.py:51
  50.8 1.5 %collective-permute-start.17 = (bf16[1,128,1024]{2,1,0:T(8,128)(2,1)S(1)}, bf16[1,128,1024]{2,1,0:T(8,128)(2,1)S(1)}, u32[]{:S(2)}, u32[]{:S(2)}) collective-permute-start(bf16[1,128,1024]{2,1,0:T(8,128)(2,1)S(1)} %bitcast.12), channel_id=1, source_target_pairs={{0,4},{1,5},{2,6},{3,7},{4,0},{5,1},{6,2},{7,3},{8,12},{9,13},{10,... | collective-permute-start | bytes 786440 | tf_op jit(solution)/shard_map/ppermute | solution.py:473
  53.8 1.5 %collective-permute-start.21 = (bf16[1,128,1024]{2,1,0:T(8,128)(2,1)S(1)}, bf16[1,128,1024]{2,1,0:T(8,128)(2,1)S(1)}, u32[]{:S(2)}, u32[]{:S(2)}) collective-permute-start(bf16[1,128,1024]{2,1,0:T(8,128)(2,1)S(1)} %collective-permute-done.20.refs_4_), channel_id=1, source_target_pairs={{0,4},{1,5},{2,6},{3,7},{4,0},{5,1},{6,2},{7,3},{8,12},{9,13},{10,... | collective-permute-start | bytes 786440 | tf_op jit(solution)/shard_map/ppermute | solution.py:473
  55.4 1.2 %collective-permute-start.23 = (bf16[1,128,1024]{2,1,0:T(8,128)(2,1)S(1)}, bf16[1,128,1024]{2,1,0:T(8,128)(2,1)S(1)}, u32[]{:S(2)}, u32[]{:S(2)}) collective-permute-start(bf16[1,128,1024]{2,1,0:T(8,128)(2,1)S(1)} %collective-permute-done.22.refs_6_), channel_id=1, source_target_pairs={{0,4},{1,5},{2,6},{3,7},{4,0},{5,1},{6,2},{7,3},{8,12},{9,13},{10,... | collective-permute-start | bytes 786440 | tf_op jit(solution)/shard_map/ppermute | solution.py:473
  57.5 3.1 %shard_map.122 = (bf16[64,1024]{1,0:T(8,128)(2,1)S(1)}, bf16[4,64,128]{2,1,0:T(8,128)(2,1)S(1)}) custom-call(f32[256,512]{1,0:T(8,128)S(1)} %get-tuple-element.54.keep_ref, bf16[256,512]{1,0:T(8,128)(2,1)S(1)} %collective-permute-done.15.recv_ref, bf16[256,768]{1,0:T(8,128)(2,1)S(1)} %get-tuple-element.56.proj_mine, ...), custom_call_target="tpu_custom_call" | custom-call | flops 805306368 | bytes 2684354 | tf_op jit(solution)/shard_map/pallas_call | solution.py:51
  62.5 3.3 %collective-permute-done.19.refs_3_ = bf16[1,128,1024]{2,1,0:T(8,128)(2,1)S(1)} collective-permute-done((bf16[1,128,1024]{2,1,0:T(8,128)(2,1)S(1)}, bf16[1,128,1024]{2,1,0:T(8,128)(2,1)S(1)}, u32[]{:S(2)}, u32[]{:S(2)}) %collective-permute-start.19) | collective-permute-done | bytes 262176 | tf_op jit(solution)/shard_map/ppermute | solution.py:473
  65.8 2.3 %collective-permute-start.25 = (bf16[4,64,128]{2,1,0:T(8,128)(2,1)S(1)}, bf16[4,64,128]{2,1,0:T(8,128)(2,1)S(1)}, u32[]{:S(2)}, u32[]{:S(2)}) collective-permute-start(bf16[4,64,128]{2,1,0:T(8,128)(2,1)S(1)} %get-tuple-element.63), channel_id=1, source_target_pairs={{0,6},{1,7},{2,4},{3,5},{4,2},{5,3},{6,0},{7,1},{8,14},{9,15},{10,... | collective-permute-start | bytes 196616 | tf_op jit(solution)/shard_map/ppermute | solution.py:473
  68.1 4.6 %collective-permute-done.21.refs_5_ = bf16[1,128,1024]{2,1,0:T(8,128)(2,1)S(1)} collective-permute-done((bf16[1,128,1024]{2,1,0:T(8,128)(2,1)S(1)}, bf16[1,128,1024]{2,1,0:T(8,128)(2,1)S(1)}, u32[]{:S(2)}, u32[]{:S(2)}) %collective-permute-start.21) | collective-permute-done | bytes 262176 | tf_op jit(solution)/shard_map/ppermute | solution.py:473
  72.6 3.6 %collective-permute-done.23.refs_7_ = bf16[1,128,1024]{2,1,0:T(8,128)(2,1)S(1)} collective-permute-done((bf16[1,128,1024]{2,1,0:T(8,128)(2,1)S(1)}, bf16[1,128,1024]{2,1,0:T(8,128)(2,1)S(1)}, u32[]{:S(2)}, u32[]{:S(2)}) %collective-permute-start.23) | collective-permute-done | bytes 262176 | tf_op jit(solution)/shard_map/ppermute | solution.py:473
  77.1 1.9 %collective-permute-start.27 = (bf16[2,1,64,128]{3,2,1,0:T(8,128)(2,1)S(1)}, bf16[2,1,64,128]{3,2,1,0:T(8,128)(2,1)S(1)}, u32[]{:S(2)}, u32[]{:S(2)}) collective-permute-start(bf16[2,1,64,128]{3,2,1,0:T(8,128)(2,1)S(1)} %get-tuple-element.74), channel_id=1, source_target_pairs={{0,8},{1,9},{2,10},{3,11},{4,12},{5,13},{6,14},{7,15},{8,16},{9,17... | collective-permute-start | bytes 98312 | tf_op jit(solution)/shard_map/ppermute | solution.py:473
  78.9 2.6 %collective-permute-start.28 = (bf16[2,1,64,128]{3,2,1,0:T(8,128)(2,1)S(1)}, bf16[2,1,64,128]{3,2,1,0:T(8,128)(2,1)S(1)}, u32[]{:S(2)}, u32[]{:S(2)}) collective-permute-start(bf16[2,1,64,128]{3,2,1,0:T(8,128)(2,1)S(1)} %get-tuple-element.75), channel_id=1, source_target_pairs={{0,16},{1,17},{2,18},{3,19},{4,20},{5,21},{6,22},{7,23},{8,24},{9,... | collective-permute-start | bytes 98312 | tf_op jit(solution)/shard_map/ppermute | solution.py:473
  81.5 1.3 %collective-permute-start.29 = (bf16[2,1,64,128]{3,2,1,0:T(8,128)(2,1)S(1)}, bf16[2,1,64,128]{3,2,1,0:T(8,128)(2,1)S(1)}, u32[]{:S(2)}, u32[]{:S(2)}) collective-permute-start(bf16[2,1,64,128]{3,2,1,0:T(8,128)(2,1)S(1)} %get-tuple-element.76), channel_id=1, source_target_pairs={{0,24},{1,25},{2,26},{3,27},{4,28},{5,29},{6,30},{7,31},{8,0},{9,1... | collective-permute-start | bytes 98312 | tf_op jit(solution)/shard_map/ppermute | solution.py:473
  84.2 1.3 %collective-permute-done.29.refs_11_ = bf16[2,1,64,128]{3,2,1,0:T(8,128)(2,1)S(1)} collective-permute-done((bf16[2,1,64,128]{3,2,1,0:T(8,128)(2,1)S(1)}, bf16[2,1,64,128]{3,2,1,0:T(8,128)(2,1)S(1)}, u32[]{:S(2)}, u32[]{:S(2)}) %collective-permute-start.29) | collective-permute-done | bytes 32800 | tf_op jit(solution)/shard_map/ppermute | solution.py:473
  86.7 1.7 %shard_map.125 = f32[1024,128]{1,0:T(8,128)} custom-call(bf16[1,128,1024]{2,1,0:T(8,128)(2,1)S(1)} %bitcast.13, bf16[1,128,1024]{2,1,0:T(8,128)(2,1)S(1)} %collective-permute-done.17.refs_1_, bf16[1,128,1024]{2,1,0:T(8,128)(2,1)S(1)} %collective-permute-done.18.refs_2_, bf16[1,128,1024]{2,1,0:T(8,128)(2,1)S(1)} %collective-permute-done.19.refs_3_, ...), custom_call_target="tpu_custom_call" | custom-call | flops 268435456 | bytes 894784 | tf_op jit(solution)/shard_map/pallas_call | solution.py:51
  88.3 1.5 %shard_map.124 = bf16[128,1024]{1,0:T(8,128)(2,1)} custom-call(bf16[64,1024]{1,0:T(8,128)(2,1)S(1)} %get-tuple-element.64.mine_ref, bf16[64,1024]{1,0:T(8,128)(2,1)S(1)} %collective-permute-done.26.pair_ref, bf16[1024,1024]{1,0:T(8,128)(2,1)S(1)} %copy-done.2), custom_call_target="tpu_custom_call" | custom-call | flops 268435456 | bytes 894784 | tf_op jit(solution)/shard_map/pallas_call | solution.py:51
  (70 shorter events, 16.0 us)
Async XLA Ops:
  0.6 39.0 %collective-permute-start.12 = (bf16[4,1024,512]{2,1,0:T(8,128)(2,1)}, bf16[4,1024,512]{2,1,0:T(8,128)(2,1)S(1)}, u32[]{:S(2)}, u32[]{:S(2)}) collective-permute-start(bf16[4,1024,512]{2,1,0:T(8,128)(2,1)} %head_mine.3), channel_id=1, source_target_pairs={{0,1},{1,0},{2,3},{3,2},{4,5},{5,4},{6,7},{7,6},{8,9},{9,8},{10,11... | collective-permute-start | bytes 12582920 | tf_op jit(solution)/shard_map/ppermute | solution.py:465
  1.2 26.8 %collective-permute-start.5 = (bf16[3,1024,256]{2,1,0:T(8,128)(2,1)}, bf16[3,1024,256]{2,1,0:T(8,128)(2,1)S(1)}, u32[]{:S(2)}, u32[]{:S(2)}) collective-permute-start(bf16[3,1024,256]{2,1,0:T(8,128)(2,1)} %bitcast.6), channel_id=1, source_target_pairs={{0,1},{1,0},{2,3},{3,2},{4,5},{5,4},{6,7},{7,6},{8,9},{9,8},{10,11... | collective-permute-start | bytes 4718600 | tf_op jit(solution)/shard_map/ppermute | solution.py:465
  4.7 5.9 %collective-permute-start.2 = (bf16[3,64,256]{2,1,0:T(8,128)(2,1)S(1)}, bf16[3,64,256]{2,1,0:T(8,128)(2,1)S(1)}, u32[]{:S(2)}, u32[]{:S(2)}) collective-permute-start(bf16[3,64,256]{2,1,0:T(8,128)(2,1)S(1)} %get-tuple-element.43), channel_id=1, source_target_pairs={{0,1},{1,0},{2,3},{3,2},{4,5},{5,4},{6,7},{7,6},{8,9},{9,8},{10,11... | collective-permute-start | bytes 294920 | tf_op jit(solution)/shard_map/ppermute | solution.py:465
  5.2 9.8 %collective-permute-start.8 = (bf16[128,1024]{1,0:T(8,128)(2,1)S(1)}, bf16[128,1024]{1,0:T(8,128)(2,1)S(1)}, u32[]{:S(2)}, u32[]{:S(2)}) collective-permute-start(bf16[128,1024]{1,0:T(8,128)(2,1)S(1)} %shard_map.116), channel_id=1, source_target_pairs={{0,2},{1,3},{2,0},{3,1},{4,6},{5,7},{6,4},{7,5},{8,10},{9,11},{10,... | collective-permute-start | bytes 786440 | tf_op jit(solution)/shard_map/ppermute | solution.py:465
  8.4 9.4 %collective-permute-start = (bf16[64,1024]{1,0:T(8,128)(2,1)S(1)}, bf16[64,1024]{1,0:T(8,128)(2,1)S(1)}, u32[]{:S(2)}, u32[]{:S(2)}) collective-permute-start(bf16[64,1024]{1,0:T(8,128)(2,1)S(1)} %get-tuple-element.41), channel_id=1, source_target_pairs={{0,1},{1,0},{2,3},{3,2},{4,5},{5,4},{6,7},{7,6},{8,9},{9,8},{10,11... | collective-permute-start | bytes 393224 | tf_op jit(solution)/shard_map/ppermute | solution.py:465
  10.6 6.3 %collective-permute-start.3 = (bf16[3,64,256]{2,1,0:T(8,128)(2,1)S(1)}, bf16[3,64,256]{2,1,0:T(8,128)(2,1)S(1)}, u32[]{:S(2)}, u32[]{:S(2)}) collective-permute-start(bf16[3,64,256]{2,1,0:T(8,128)(2,1)S(1)} %get-tuple-element.42.look0), channel_id=1, source_target_pairs={{0,2},{1,3},{2,0},{3,1},{4,6},{5,7},{6,4},{7,5},{8,10},{9,11},{10,... | collective-permute-start | bytes 294920 | tf_op jit(solution)/shard_map/ppermute | solution.py:465
  15.0 12.4 %collective-permute-start.9 = (bf16[128,1024]{1,0:T(8,128)(2,1)S(1)}, bf16[128,1024]{1,0:T(8,128)(2,1)S(1)}, u32[]{:S(2)}, u32[]{:S(2)}) collective-permute-start(bf16[128,1024]{1,0:T(8,128)(2,1)S(1)} %collective-permute-done.8.part_a), channel_id=1, source_target_pairs={{0,4},{1,5},{2,6},{3,7},{4,0},{5,1},{6,2},{7,3},{8,12},{9,13},{10,... | collective-permute-start | bytes 786440 | tf_op jit(solution)/shard_map/ppermute | solution.py:473
  16.8 4.8 %collective-permute-start.4 = (bf16[3,64,256]{2,1,0:T(8,128)(2,1)S(1)}, bf16[3,64,256]{2,1,0:T(8,128)(2,1)S(1)}, u32[]{:S(2)}, u32[]{:S(2)}) collective-permute-start(bf16[3,64,256]{2,1,0:T(8,128)(2,1)S(1)} %get-tuple-element.43), channel_id=1, source_target_pairs={{0,3},{1,2},{2,1},{3,0},{4,7},{5,6},{6,5},{7,4},{8,11},{9,10},{10,... | collective-permute-start | bytes 294920 | tf_op jit(solution)/shard_map/ppermute | solution.py:465
  17.8 16.5 %collective-permute-start.7 = (bf16[256,1024]{1,0:T(8,128)(2,1)S(1)}, bf16[256,1024]{1,0:T(8,128)(2,1)S(1)}, u32[]{:S(2)}, u32[]{:S(2)}) collective-permute-start(bf16[256,1024]{1,0:T(8,128)(2,1)S(1)} %copy-done.3), channel_id=1, source_target_pairs={{0,1},{1,0},{2,3},{3,2},{4,5},{5,4},{6,7},{7,6},{8,9},{9,8},{10,11... | collective-permute-start | bytes 1572872 | tf_op jit(solution)/shard_map/ppermute | solution.py:465
  21.6 5.8 %collective-permute-start.1 = (bf16[64,1024]{1,0:T(8,128)(2,1)S(1)}, bf16[64,1024]{1,0:T(8,128)(2,1)S(1)}, u32[]{:S(2)}, u32[]{:S(2)}) collective-permute-start(bf16[64,1024]{1,0:T(8,128)(2,1)S(1)} %shard_map.113.own_ref), channel_id=1, source_target_pairs={{0,2},{1,3},{2,0},{3,1},{4,6},{5,7},{6,4},{7,5},{8,10},{9,11},{10,... | collective-permute-start | bytes 393224 | tf_op jit(solution)/shard_map/ppermute | solution.py:465
  27.5 5.2 %collective-permute-start.10 = (bf16[128,1024]{1,0:T(8,128)(2,1)S(1)}, bf16[128,1024]{1,0:T(8,128)(2,1)S(1)}, u32[]{:S(2)}, u32[]{:S(2)}) collective-permute-start(bf16[128,1024]{1,0:T(8,128)(2,1)S(1)} %collective-permute-done.8.part_a), channel_id=1, source_target_pairs={{0,1},{1,0},{2,3},{3,2},{4,5},{5,4},{6,7},{7,6},{8,9},{9,8},{10,11... | collective-permute-start | bytes 786440 | tf_op jit(solution)/shard_map/ppermute | solution.py:465
  27.5 9.4 %collective-permute-start.11 = (bf16[128,1024]{1,0:T(8,128)(2,1)S(1)}, bf16[128,1024]{1,0:T(8,128)(2,1)S(1)}, u32[]{:S(2)}, u32[]{:S(2)}) collective-permute-start(bf16[128,1024]{1,0:T(8,128)(2,1)S(1)} %collective-permute-done.9.part_b), channel_id=1, source_target_pairs={{0,1},{1,0},{2,3},{3,2},{4,5},{5,4},{6,7},{7,6},{8,9},{9,8},{10,11... | collective-permute-start | bytes 786440 | tf_op jit(solution)/shard_map/ppermute | solution.py:465
  31.3 8.3 %collective-permute-start.6 = (bf16[256,512]{1,0:T(8,128)(2,1)S(1)}, bf16[256,512]{1,0:T(8,128)(2,1)S(1)}, u32[]{:S(2)}, u32[]{:S(2)}) collective-permute-start(bf16[256,512]{1,0:T(8,128)(2,1)S(1)} %get-tuple-element.44.att_ref), channel_id=1, source_target_pairs={{0,2},{1,3},{2,0},{3,1},{4,6},{5,7},{6,4},{7,5},{8,10},{9,11},{10,... | collective-permute-start | bytes 786440 | tf_op jit(solution)/shard_map/ppermute | solution.py:465
  32.7 19.7 %collective-permute-start.18 = (bf16[1,128,1024]{2,1,0:T(8,128)(2,1)S(1)}, bf16[1,128,1024]{2,1,0:T(8,128)(2,1)S(1)}, u32[]{:S(2)}, u32[]{:S(2)}) collective-permute-start(bf16[1,128,1024]{2,1,0:T(8,128)(2,1)S(1)} %bitcast.9), channel_id=1, source_target_pairs={{0,8},{1,9},{2,10},{3,11},{4,12},{5,13},{6,14},{7,15},{8,16},{9,17... | collective-permute-start | bytes 786440 | tf_op jit(solution)/shard_map/ppermute | solution.py:473
  34.2 19.6 %collective-permute-start.20 = (bf16[1,128,1024]{2,1,0:T(8,128)(2,1)S(1)}, bf16[1,128,1024]{2,1,0:T(8,128)(2,1)S(1)}, u32[]{:S(2)}, u32[]{:S(2)}) collective-permute-start(bf16[1,128,1024]{2,1,0:T(8,128)(2,1)S(1)} %bitcast.10), channel_id=1, source_target_pairs={{0,16},{1,17},{2,18},{3,19},{4,20},{5,21},{6,22},{7,23},{8,24},{9,... | collective-permute-start | bytes 786440 | tf_op jit(solution)/shard_map/ppermute | solution.py:473
  36.8 17.0 %collective-permute-start.22 = (bf16[1,128,1024]{2,1,0:T(8,128)(2,1)S(1)}, bf16[1,128,1024]{2,1,0:T(8,128)(2,1)S(1)}, u32[]{:S(2)}, u32[]{:S(2)}) collective-permute-start(bf16[1,128,1024]{2,1,0:T(8,128)(2,1)S(1)} %bitcast.11), channel_id=1, source_target_pairs={{0,24},{1,25},{2,26},{3,27},{4,28},{5,29},{6,30},{7,31},{8,0},{9,1... | collective-permute-start | bytes 786440 | tf_op jit(solution)/shard_map/ppermute | solution.py:473
  43.1 4.1 %collective-permute-start.13 = (f32[64,128]{1,0:T(8,128)S(1)}, f32[64,128]{1,0:T(8,128)S(1)}, u32[]{:S(2)}, u32[]{:S(2)}) collective-permute-start(f32[64,128]{1,0:T(8,128)S(1)} %get-tuple-element.50.stats_ref), channel_id=1, source_target_pairs={{0,2},{1,3},{2,0},{3,1},{4,6},{5,7},{6,4},{7,5},{8,10},{9,11},{10,... | collective-permute-start | bytes 98312 | tf_op jit(solution)/shard_map/ppermute | solution.py:465
  49.6 7.9 %collective-permute-start.15 = (bf16[256,512]{1,0:T(8,128)(2,1)S(1)}, bf16[256,512]{1,0:T(8,128)(2,1)S(1)}, u32[]{:S(2)}, u32[]{:S(2)}) collective-permute-start(bf16[256,512]{1,0:T(8,128)(2,1)S(1)} %get-tuple-element.55), channel_id=1, source_target_pairs={{0,2},{1,3},{2,0},{3,1},{4,6},{5,7},{6,4},{7,5},{8,10},{9,11},{10,... | collective-permute-start | bytes 786440 | tf_op jit(solution)/shard_map/ppermute | solution.py:465
  50.8 10.9 %collective-permute-start.17 = (bf16[1,128,1024]{2,1,0:T(8,128)(2,1)S(1)}, bf16[1,128,1024]{2,1,0:T(8,128)(2,1)S(1)}, u32[]{:S(2)}, u32[]{:S(2)}) collective-permute-start(bf16[1,128,1024]{2,1,0:T(8,128)(2,1)S(1)} %bitcast.12), channel_id=1, source_target_pairs={{0,4},{1,5},{2,6},{3,7},{4,0},{5,1},{6,2},{7,3},{8,12},{9,13},{10,... | collective-permute-start | bytes 786440 | tf_op jit(solution)/shard_map/ppermute | solution.py:473
  52.3 13.5 %collective-permute-start.19 = (bf16[1,128,1024]{2,1,0:T(8,128)(2,1)S(1)}, bf16[1,128,1024]{2,1,0:T(8,128)(2,1)S(1)}, u32[]{:S(2)}, u32[]{:S(2)}) collective-permute-start(bf16[1,128,1024]{2,1,0:T(8,128)(2,1)S(1)} %collective-permute-done.18.refs_2_), channel_id=1, source_target_pairs={{0,4},{1,5},{2,6},{3,7},{4,0},{5,1},{6,2},{7,3},{8,12},{9,13},{10,... | collective-permute-start | bytes 786440 | tf_op jit(solution)/shard_map/ppermute | solution.py:473
  53.8 1.5 %collective-permute-start.14 = (f32[64,128]{1,0:T(8,128)S(1)}, f32[64,128]{1,0:T(8,128)S(1)}, u32[]{:S(2)}, u32[]{:S(2)}) collective-permute-start(f32[64,128]{1,0:T(8,128)S(1)} %get-tuple-element.52.loss_mine), channel_id=1, source_target_pairs={{0,1},{1,0},{2,3},{3,2},{4,5},{5,4},{6,7},{7,6},{8,9},{9,8},{10,11... | collective-permute-start | bytes 98312 | tf_op jit(solution)/shard_map/ppermute | solution.py:465
  53.8 18.8 %collective-permute-start.21 = (bf16[1,128,1024]{2,1,0:T(8,128)(2,1)S(1)}, bf16[1,128,1024]{2,1,0:T(8,128)(2,1)S(1)}, u32[]{:S(2)}, u32[]{:S(2)}) collective-permute-start(bf16[1,128,1024]{2,1,0:T(8,128)(2,1)S(1)} %collective-permute-done.20.refs_4_), channel_id=1, source_target_pairs={{0,4},{1,5},{2,6},{3,7},{4,0},{5,1},{6,2},{7,3},{8,12},{9,13},{10,... | collective-permute-start | bytes 786440 | tf_op jit(solution)/shard_map/ppermute | solution.py:473
  55.4 20.8 %collective-permute-start.23 = (bf16[1,128,1024]{2,1,0:T(8,128)(2,1)S(1)}, bf16[1,128,1024]{2,1,0:T(8,128)(2,1)S(1)}, u32[]{:S(2)}, u32[]{:S(2)}) collective-permute-start(bf16[1,128,1024]{2,1,0:T(8,128)(2,1)S(1)} %collective-permute-done.22.refs_6_), channel_id=1, source_target_pairs={{0,4},{1,5},{2,6},{3,7},{4,0},{5,1},{6,2},{7,3},{8,12},{9,13},{10,... | collective-permute-start | bytes 786440 | tf_op jit(solution)/shard_map/ppermute | solution.py:473
  60.6 15.6 %collective-permute-start.16 = (bf16[64,1024]{1,0:T(8,128)(2,1)S(1)}, bf16[64,1024]{1,0:T(8,128)(2,1)S(1)}, u32[]{:S(2)}, u32[]{:S(2)}) collective-permute-start(bf16[64,1024]{1,0:T(8,128)(2,1)S(1)} %get-tuple-element.61.refs_0_), channel_id=1, source_target_pairs={{0,2},{1,3},{2,0},{3,1},{4,6},{5,7},{6,4},{7,5},{8,10},{9,11},{10,... | collective-permute-start | bytes 393224 | tf_op jit(solution)/shard_map/ppermute | solution.py:465
  61.7 15.2 %collective-permute-start.24 = (bf16[4,64,128]{2,1,0:T(8,128)(2,1)S(1)}, bf16[4,64,128]{2,1,0:T(8,128)(2,1)S(1)}, u32[]{:S(2)}, u32[]{:S(2)}) collective-permute-start(bf16[4,64,128]{2,1,0:T(8,128)(2,1)S(1)} %get-tuple-element.63), channel_id=1, source_target_pairs={{0,4},{1,5},{2,6},{3,7},{4,0},{5,1},{6,2},{7,3},{8,12},{9,13},{10,... | collective-permute-start | bytes 196616 | tf_op jit(solution)/shard_map/ppermute | solution.py:473
  65.8 11.1 %collective-permute-start.25 = (bf16[4,64,128]{2,1,0:T(8,128)(2,1)S(1)}, bf16[4,64,128]{2,1,0:T(8,128)(2,1)S(1)}, u32[]{:S(2)}, u32[]{:S(2)}) collective-permute-start(bf16[4,64,128]{2,1,0:T(8,128)(2,1)S(1)} %get-tuple-element.63), channel_id=1, source_target_pairs={{0,6},{1,7},{2,4},{3,5},{4,2},{5,3},{6,0},{7,1},{8,14},{9,15},{10,... | collective-permute-start | bytes 196616 | tf_op jit(solution)/shard_map/ppermute | solution.py:473
  77.0 11.3 %collective-permute-start.26 = (bf16[64,1024]{1,0:T(8,128)(2,1)S(1)}, bf16[64,1024]{1,0:T(8,128)(2,1)S(1)}, u32[]{:S(2)}, u32[]{:S(2)}) collective-permute-start(bf16[64,1024]{1,0:T(8,128)(2,1)S(1)} %get-tuple-element.64.mine_ref), channel_id=1, source_target_pairs={{0,1},{1,0},{2,3},{3,2},{4,5},{5,4},{6,7},{7,6},{8,9},{9,8},{10,11... | collective-permute-start | bytes 393224 | tf_op jit(solution)/shard_map/ppermute | solution.py:465
  77.1 5.9 %collective-permute-start.27 = (bf16[2,1,64,128]{3,2,1,0:T(8,128)(2,1)S(1)}, bf16[2,1,64,128]{3,2,1,0:T(8,128)(2,1)S(1)}, u32[]{:S(2)}, u32[]{:S(2)}) collective-permute-start(bf16[2,1,64,128]{3,2,1,0:T(8,128)(2,1)S(1)} %get-tuple-element.74), channel_id=1, source_target_pairs={{0,8},{1,9},{2,10},{3,11},{4,12},{5,13},{6,14},{7,15},{8,16},{9,17... | collective-permute-start | bytes 98312 | tf_op jit(solution)/shard_map/ppermute | solution.py:473
  78.9 5.2 %collective-permute-start.28 = (bf16[2,1,64,128]{3,2,1,0:T(8,128)(2,1)S(1)}, bf16[2,1,64,128]{3,2,1,0:T(8,128)(2,1)S(1)}, u32[]{:S(2)}, u32[]{:S(2)}) collective-permute-start(bf16[2,1,64,128]{3,2,1,0:T(8,128)(2,1)S(1)} %get-tuple-element.75), channel_id=1, source_target_pairs={{0,16},{1,17},{2,18},{3,19},{4,20},{5,21},{6,22},{7,23},{8,24},{9,... | collective-permute-start | bytes 98312 | tf_op jit(solution)/shard_map/ppermute | solution.py:473
  81.5 3.9 %collective-permute-start.29 = (bf16[2,1,64,128]{3,2,1,0:T(8,128)(2,1)S(1)}, bf16[2,1,64,128]{3,2,1,0:T(8,128)(2,1)S(1)}, u32[]{:S(2)}, u32[]{:S(2)}) collective-permute-start(bf16[2,1,64,128]{3,2,1,0:T(8,128)(2,1)S(1)} %get-tuple-element.76), channel_id=1, source_target_pairs={{0,24},{1,25},{2,26},{3,27},{4,28},{5,29},{6,30},{7,31},{8,0},{9,1... | collective-permute-start | bytes 98312 | tf_op jit(solution)/shard_map/ppermute | solution.py:473
  82.9 2.6 %collective-permute-start.30 = (bf16[2,1,64,128]{3,2,1,0:T(8,128)(2,1)S(1)}, bf16[2,1,64,128]{3,2,1,0:T(8,128)(2,1)S(1)}, u32[]{:S(2)}, u32[]{:S(2)}) collective-permute-start(bf16[2,1,64,128]{3,2,1,0:T(8,128)(2,1)S(1)} %get-tuple-element.73.refs_8_), channel_id=1, source_target_pairs={{0,1},{1,0},{2,3},{3,2},{4,5},{5,4},{6,7},{7,6},{8,9},{9,8},{10,11... | collective-permute-start | bytes 98312 | tf_op jit(solution)/shard_map/ppermute | solution.py:465
  83.0 2.5 %collective-permute-start.31 = (bf16[2,1,64,128]{3,2,1,0:T(8,128)(2,1)S(1)}, bf16[2,1,64,128]{3,2,1,0:T(8,128)(2,1)S(1)}, u32[]{:S(2)}, u32[]{:S(2)}) collective-permute-start(bf16[2,1,64,128]{3,2,1,0:T(8,128)(2,1)S(1)} %collective-permute-done.27.refs_9_), channel_id=1, source_target_pairs={{0,1},{1,0},{2,3},{3,2},{4,5},{5,4},{6,7},{7,6},{8,9},{9,8},{10,11... | collective-permute-start | bytes 98312 | tf_op jit(solution)/shard_map/ppermute | solution.py:465
  (12 other events, 86.8 us)
